TPU v7x, 32 devices: a whole 2x2x4 slice. The times are simulated.
32 devices in a mesh: strip: 2 (over x), az: 4 (over z), tile: 4 (over y, core).
Axes of the slice: x: 2, y: 2, z: 4, core: 2. Of those that a mesh axis runs over, the one named last changes fastest.
Arguments:
- raw_echo: float32 [2, 4096, 4096], P(None, ('strip', 'az', 'tile')), parts along dimension 1, may hold values from -6 to 6
- phase_scaling: float32 [1024, 4096], P(None, 'tile'), may hold values from -3.140625 to 3.140625
- phase_range: float32 [1024, 4096], P('tile'), may hold values from -3.140625 to 3.140625
- phase_azimuth: float32 [1024, 4096], P(None, 'tile'), may hold values from -3.140625 to 3.140625
Outputs:
- image: float32 [2, 4096, 4096], P(None, ('strip', 'az'), 'tile'), parts along dimension 1
There are 2 independent parts, one for each index of `strip`. A program takes and returns all parts, laid end to end along the dimension named above; an argument that names none is the same for every part. Nothing has to cross between parts.
All inputs are finite; a program needn't handle non-finite values.
Results may differ from a plain program's by a relative error of at most 0.00007.
Values sent between devices are 32-bit elements; how exact they have to be, the bound alone decides.
A program may use at most 128 MiB of HBM per device.

v0:
```python
import functools
import math

import jax
import jax.numpy as jnp
import numpy as np
from jax import lax
from jax.experimental import pallas as pl
from jax.experimental.pallas import tpu as pltpu
from jax.sharding import PartitionSpec as P

F32 = jnp.float32
BF16 = jnp.bfloat16
LANES = 128


def halves(table):
    hi = np.asarray(table, np.float32).astype(jnp.bfloat16)
    lo = (np.asarray(table, np.float64) - hi.astype(np.float64)).astype(jnp.bfloat16)
    return np.stack([hi, lo])


def roots(rows, cols, modulus, direction):
    residue = np.outer(rows, cols) % modulus
    angle = residue * (direction * 2.0 * math.pi / modulus)
    return np.cos(angle), np.sin(angle)


def left_table(rows, cols, modulus, direction, scale=1.0):
    c, s = roots(rows, cols, modulus, direction)
    return halves(np.block([[c, -s], [s, c]]) * scale)


def right_table(rows, cols, modulus, direction, scale=1.0):
    c, s = roots(rows, cols, modulus, direction)
    return halves(np.block([[c, s], [-s, c]]) * scale)


def twist_table(count, length, modulus, direction):
    c, s = roots(np.arange(count), np.arange(length), modulus, direction)
    full = np.stack([c, s]).astype(np.float32)
    return np.ascontiguousarray(np.broadcast_to(full[..., None], full.shape + (LANES,)))


def split(x):
    hi = x.astype(BF16)
    return hi, (x - hi.astype(F32)).astype(BF16)


def mm(a, b):
    return jnp.dot(a, b, preferred_element_type=F32)


def times(a, t):
    return a[0] * t[0] - a[1] * t[1], a[0] * t[1] + a[1] * t[0]


def plus(a, b):
    return a[0] + b[0], a[1] + b[1]


def minus(a, b):
    return a[0] - b[0], a[1] - b[1]


def quarter(a, direction):
    return (-a[1], a[0]) if direction > 0 else (a[1], -a[0])


def four(v, direction):
    a, b = plus(v[0], v[2]), minus(v[0], v[2])
    c, d = plus(v[1], v[3]), quarter(minus(v[1], v[3]), direction)
    return [plus(a, c), plus(b, d), minus(a, c), minus(b, d)]


def fft(v, direction):
    n = len(v)
    if n == 1:
        return v
    if n == 2:
        return [plus(v[0], v[1]), minus(v[0], v[1])]
    if n == 4:
        return four(v, direction)
    parts = [fft(v[e::4], direction) for e in range(4)] if n % 4 == 0 else None
    out = [None] * n
    m = n // 4
    for f in range(m):
        items = []
        for e in range(4):
            x = parts[e][f]
            k = e * f % n
            if k == 0:
                pass
            elif 8 * k == n:
                h = np.float32(math.sqrt(0.5))
                q = quarter(x, direction)
                x = ((x[0] + q[0]) * h, (x[1] + q[1]) * h)
            elif 4 * k == n:
                x = quarter(x, direction)
            elif 8 * k == 3 * n:
                h = np.float32(math.sqrt(0.5))
                q = quarter(x, direction)
                x = ((q[0] - x[0]) * h, (q[1] - x[1]) * h)
            else:
                ang = direction * 2.0 * math.pi * k / n
                x = times(x, (np.float32(math.cos(ang)), np.float32(math.sin(ang))))
            items.append(x)
        got = four(items, direction)
        for j in range(4):
            out[f + j * m] = got[j]
    return out


def sincos(x):
    y = x * 0.5
    z = y * y
    s, c = -1.0 / 39916800, 1.0 / 479001600
    for a, b in ((362880, -3628800), (-5040, 40320), (120, -720), (-6, 24), (1, -2)):
        s = s * z + np.float32(1.0 / a)
        c = c * z + np.float32(1.0 / b)
    s = s * y
    c = c * z + 1.0
    return 1.0 - 2.0 * s * s, 2.0 * s * c


def greet(partners):
    barrier = pltpu.get_barrier_semaphore()
    for device in partners:
        pl.semaphore_signal(barrier, inc=1, device_id=device, device_id_type=pl.DeviceIdType.MESH)
    return barrier


def lanes(j):
    return pl.ds(pl.multiple_of(j * LANES, LANES), LANES)


def filter_rows(x_ref, base, block, fwd_ref, inv_ref, twist_ref, phase_ref, hi_ref, lo_ref, mid_ref):
    n_one = phase_ref.shape[0]
    step = 16
    f_hi, f_lo = fwd_ref[0], fwd_ref[1]
    b_hi, b_lo = inv_ref[0], inv_ref[1]

    @pl.loop(0, block // step)
    def _(i):
        rows = pl.ds(pl.multiple_of(i * step, step), step)
        at = pl.ds(pl.multiple_of(base + i * step, step), step)
        v = [
            tuple(x_ref[c, at, pl.ds(a * LANES, LANES)] for c in (0, 1))
            for a in range(n_one)
        ]
        for k, x in enumerate(fft(v, -1)):
            if k:
                x = times(x, (twist_ref[0, k : k + 1, :], twist_ref[1, k : k + 1, :]))
            for c in (0, 1):
                h, l = split(x[c])
                hi_ref[k, rows, pl.ds(c * LANES, LANES)] = h
                lo_ref[k, rows, pl.ds(c * LANES, LANES)] = l

    group = 4

    @pl.loop(0, n_one // group)
    def _(i):
        ks = pl.ds(i * group, group)
        flat = (group * block, 2 * LANES)
        h, l = hi_ref[ks].reshape(flat), lo_ref[ks].reshape(flat)
        r = mm(h, f_hi) + mm(l, f_hi) + mm(h, f_lo)
        turn = phase_ref[ks, pl.ds(pl.multiple_of(base, block), block), :]
        r = times((r[:, :LANES], r[:, LANES:]), sincos(turn.reshape(group * block, LANES)))
        h, l = split(jnp.concatenate(r, axis=1))
        r = mm(h, b_hi) + mm(l, b_hi) + mm(h, b_lo)
        at = pl.ds(pl.multiple_of(i * group * block, block), group * block)
        mid_ref[0, at, :] = r[:, :LANES]
        mid_ref[1, at, :] = r[:, LANES:]

    @pl.loop(0, block // 8)
    def _(i):
        at = pl.ds(pl.multiple_of(base + i * 8, 8), 8)
        v = []
        for k in range(n_one):
            x = tuple(mid_ref[c, pl.ds(pl.multiple_of(k * block + i * 8, 8), 8), :] for c in (0, 1))
            if k:
                x = times(x, (twist_ref[0, k : k + 1, :], -twist_ref[1, k : k + 1, :]))
            v.append(x)
        for a, x in enumerate(fft(v, 1)):
            for c in (0, 1):
                x_ref[c, at, pl.ds(a * LANES, LANES)] = x[c]


def permute_turn(o_ref, mid, turn):
    n_one, count, _ = turn.shape
    half = mid.shape[1]
    some = min(count, LANES)
    part = half // n_one

    @pl.loop(0, count // some)
    def _(i):
        @pl.loop(0, n_one)
        def _(g):
            c, row, j = piece(g, count, o_ref)
            at = pl.ds(pl.multiple_of(row + i * some, some), some)
            x = o_ref[c, at, lanes(j)]
            if some < LANES:
                x = jnp.concatenate([x] * (LANES // some), axis=0)
            per = half // LANES
            mid[g // per, pl.ds(pl.multiple_of(g % per * LANES, LANES), LANES), :] = x.T

        @pl.loop(0, n_one)
        def _(k):
            rows = pl.ds(k, part, stride=n_one)
            x = jnp.concatenate([mid[h, rows, :] for h in range(LANES // part)], axis=0)
            at = pl.ds(pl.multiple_of(i * some, some), some)
            turn[k, at, :] = x.T[:some]


def piece(g, count, o_ref):
    across = o_ref.shape[2] // LANES
    down = o_ref.shape[1] // count
    return g // (across * down), g // across % down * count, g % across


def focus_kernel(
    tiles, length, block,
    raw_ref, scaling_ref, range_ref, azimuth_ref,
    front_ref, twist_ref, fwd_ref, inv_ref, range_twist_ref, table_ref,
    o_ref,
    spec, scaling, turn, phase, dop, ret, tail_out, tail_in, head, hi_ref, lo_ref, mid,
    send_e, recv_e, local_e, send_a, recv_a, local_a, send_b, recv_b, local_b,
    send_c, recv_c, load, load_range,
):
    me = lax.axis_index("tile")
    az = lax.axis_index("az")
    count = dop.shape[1]
    width = o_ref.shape[2]
    pulses = o_ref.shape[1]
    tail = tail_in.shape[2]
    rows_own = raw_ref.shape[1]
    n_one = turn.shape[0]
    blocks = count // block
    early = (blocks - 1) * block
    spans = width // LANES
    cols = tail_out
    m = spec.shape[1] // 4
    q = pulses // 4
    mine = pl.ds(pl.multiple_of(me * width, LANES), width)
    own = pl.ds(pl.multiple_of(me * count, count), count)
    own_pulses = pl.ds(pl.multiple_of(me * rows_own, rows_own), rows_own)

    def remote(src, dst, send, recv, device):
        return pltpu.make_async_remote_copy(
            src_ref=src, dst_ref=dst, send_sem=send, recv_sem=recv,
            device_id=device, device_id_type=pl.DeviceIdType.MESH,
        )

    def echo(j, k):
        to = lax.rem(me + k, tiles)
        return remote(
            raw_ref.at[:, :, lanes(to * spans + j)], cols.at[j, :, own_pulses, :],
            send_e.at[j, k - 1], recv_e.at[j, k - 1], {"tile": to},
        )

    def keep_echo(j):
        return pltpu.make_async_copy(
            raw_ref.at[:, :, lanes(me * spans + j)], cols.at[j, :, own_pulses, :], local_e.at[j]
        )

    def load_piece(g):
        c, row, j = piece(g, count, o_ref)
        return pltpu.make_async_copy(
            range_ref.at[:, lanes(g)],
            o_ref.at[c, pl.ds(pl.multiple_of(row, count), count), lanes(j)],
            load_range.at[g],
        )

    def out_part(i, k, lo, n, slot):
        to = lax.rem(me + k, tiles)
        at = pl.ds(pl.multiple_of(me * width + lo, LANES), n)
        return remote(
            spec.at[:, pl.ds(pl.multiple_of(to * count + i * block, block), block), pl.ds(lo, n)],
            dop.at[:, pl.ds(pl.multiple_of(i * block, block), block), at],
            send_a.at[slot, k - 1], recv_a.at[slot, k - 1], {"tile": to},
        )

    def out(i, k):
        return out_part(i, k, 0, width, i)

    def first_out(k):
        return out_part(0, k, 0, width - LANES, blocks)

    def last_out(k):
        return out_part(0, k, width - LANES, LANES, 0)

    def back_rows(j, k, lo, n, slot):
        to = lax.rem(me + k, tiles)
        return remote(
            dop.at[:, pl.ds(lo, n), lanes(to * spans + j)],
            ret.at[j, :, pl.ds(pl.multiple_of(me * count + lo, 8), n), :],
            send_b.at[slot, k - 1], recv_b.at[slot, k - 1], {"tile": to},
        )

    def first_rows(k):
        return back_rows(0, k, 0, early, spans)

    def last_rows(k):
        return back_rows(0, k, early, count - early, 0)

    def back(j, k):
        return back_rows(j, k, 0, count, j)

    def keep(j):
        return pltpu.make_async_copy(
            dop.at[:, :, lanes(me * spans + j)], ret.at[j, :, own, :], local_b.at[j]
        )

    def onward(j):
        return remote(
            tail_out.at[j, :, pl.ds(0, tail), :], tail_in.at[j], send_c.at[j], recv_c.at[j],
            {"az": lax.rem(az + 1, length)},
        )

    barrier = greet(
        [{"tile": lax.rem(me + k, tiles)} for k in range(1, tiles)]
        + [{"az": lax.rem(az + 1, length)}, {"az": lax.rem(az + length - 1, length)}]
    )
    get_scaling = pltpu.make_async_copy(scaling_ref, scaling, load.at[0])
    get_phase = pltpu.make_async_copy(azimuth_ref, phase, load.at[1])
    pl.semaphore_wait(barrier, tiles + 1)

    @pl.loop(0, spans)
    def _(j):
        for k in range(1, tiles):
            echo(j, k).start()
        keep_echo(j).start()

    @pl.loop(0, n_one)
    def _(g):
        load_piece(g).start()

    get_scaling.start()
    get_phase.start()

    get_scaling.wait()

    @pl.loop(0, spans)
    def _(j):
        @pl.when(j == spans - 1)
        def _():
            for k in range(1, tiles):
                first_out(k).start()

        for k in range(1, tiles):
            echo(j, k).wait_recv()
        keep_echo(j).wait()
        hi, lo = front_ref[0], front_ref[1]
        z = []
        for e in range(4):
            rows = pl.ds(e, q, stride=4)
            s = jnp.concatenate([cols[j, 0, rows, :], cols[j, 1, rows, :]], axis=0)
            s_hi, s_lo = split(s)
            r = mm(hi, s_hi) + mm(hi, s_lo) + mm(lo, s_hi)
            r = (r[:m], r[m:])
            if e:
                r = times(r, (twist_ref[0, e], -twist_ref[1, e]))
            z.append(r)
        for f, x in enumerate(four(z, -1)):
            rows = pl.ds(f * m, m)
            x = times(x, sincos(scaling[rows, lanes(j)]))
            spec[0, rows, lanes(j)] = x[0]
            spec[1, rows, lanes(j)] = x[1]

    for k in range(1, tiles):
        last_out(k).start()

    @pl.loop(1, blocks)
    def _(i):
        for k in range(1, tiles):
            out(i, k).start()

    first = pltpu.make_async_copy(spec.at[:, own, :], dop.at[:, :, mine], local_a)
    first.start()

    @pl.loop(0, n_one)
    def _(g):
        load_piece(g).wait()

    permute_turn(o_ref, mid, turn)
    first.wait()

    @pl.loop(0, blocks)
    def _(i):
        if early:
            @pl.when(i == blocks - 1)
            def _():
                for k in range(1, tiles):
                    first_rows(k).start()

        @pl.when(i == 0)
        def _():
            for k in range(1, tiles):
                first_out(k).wait_recv()
                last_out(k).wait_recv()

        @pl.when(i > 0)
        def _():
            for k in range(1, tiles):
                out(i, k).wait_recv()

        filter_rows(
            dop, i * block, block, fwd_ref, inv_ref, range_twist_ref, turn,
            hi_ref, lo_ref, mid,
        )

    for k in range(1, tiles):
        last_rows(k).start()
    keep(0).start()

    @pl.loop(1, spans)
    def _(j):
        for k in range(1, tiles):
            back(j, k).start()
        keep(j).start()

    get_phase.wait()

    @pl.loop(0, spans)
    def _(j):
        @pl.when(j == 0)
        def _():
            for k in range(1, tiles):
                if early:
                    first_rows(k).wait_recv()
                last_rows(k).wait_recv()

        @pl.when(j > 0)
        def _():
            for k in range(1, tiles):
                back(j, k).wait_recv()

        keep(j).wait()
        hi, lo = table_ref[0], table_ref[1]
        v = []
        for f in range(4):
            rows = pl.ds(f * m, m)
            v.append(times((ret[j, 0, rows, :], ret[j, 1, rows, :]), sincos(phase[rows, lanes(j)])))
        for e, x in enumerate(four(v, 1)):
            if e:
                x = times(x, (twist_ref[0, e], twist_ref[1, e]))
            s_hi, s_lo = split(jnp.concatenate(x, axis=0))
            r = mm(hi, s_hi) + mm(hi, s_lo) + mm(lo, s_hi)
            for c in (0, 1):
                head[c, pl.ds(e, q, stride=4), :] = r[c * m : c * m + q]
                tail_out[j, c, pl.ds(e, m - q, stride=4), :] = r[c * m + q : (c + 1) * m]

        @pl.when(az < length - 1)
        def _():
            onward(j).start()

        o_ref[:, :, lanes(j)] = head[...]

    @pl.when(az > 0)
    def _():
        @pl.loop(0, spans)
        def _(j):
            onward(j).wait_recv()
            o_ref[:, pl.ds(0, tail), lanes(j)] += tail_in[j]

    for k in range(1, tiles):
        first_out(k).wait_send()
        last_out(k).wait_send()

    @pl.loop(1, blocks)
    def _(i):
        for k in range(1, tiles):
            out(i, k).wait_send()

    for k in range(1, tiles):
        if early:
            first_rows(k).wait_send()
        last_rows(k).wait_send()

    @pl.loop(1, spans)
    def _(j):
        for k in range(1, tiles):
            back(j, k).wait_send()

    @pl.loop(0, spans)
    def _(j):
        for k in range(1, tiles):
            echo(j, k).wait_send()

    @pl.when(az < length - 1)
    def _():
        @pl.loop(0, spans)
        def _(j):
            onward(j).wait_send()


def body(raw_echo, phase_scaling, phase_range, phase_azimuth):
    tiles = lax.axis_size("tile")
    length = lax.axis_size("az")
    pulses = raw_echo.shape[1] * tiles
    extent, width = phase_scaling.shape
    count, ranges = phase_range.shape
    m, q, tail = extent // 4, pulses // 4, extent - pulses
    n_one, spans = ranges // LANES, width // LANES
    block = min(64, count)
    rows, lane = np.arange(m), np.arange(LANES)
    vmem = pl.BlockSpec(memory_space=pltpu.VMEM)
    anyspace = pl.BlockSpec(memory_space=pl.ANY)
    dma = pltpu.SemaphoreType.DMA
    c, s = roots(np.arange(n_one), lane, ranges, -1)
    return pl.pallas_call(
        functools.partial(focus_kernel, tiles, length, block),
        out_shape=jax.ShapeDtypeStruct((2, pulses, width), F32),
        in_specs=[anyspace] * 4 + [vmem] * 6,
        out_specs=vmem,
        scratch_shapes=[
            pltpu.VMEM((2, extent, width), F32),
            pltpu.VMEM((extent, width), F32),
            pltpu.VMEM((n_one, count, LANES), F32),
            pltpu.VMEM((extent, width), F32),
            pltpu.VMEM((2, count, ranges), F32),
            pltpu.VMEM((spans, 2, extent, LANES), F32),
            pltpu.VMEM((spans, 2, max(tail, pulses), LANES), F32),
            pltpu.VMEM((spans, 2, tail, LANES), F32),
            pltpu.VMEM((2, pulses, LANES), F32),
            pltpu.VMEM((n_one, block, 2 * LANES), BF16),
            pltpu.VMEM((n_one, block, 2 * LANES), BF16),
            pltpu.VMEM((2, n_one * block, LANES), F32),
            dma((spans, tiles - 1)),
            dma((spans, tiles - 1)),
            dma((spans,)),
            dma((count // block + 1, tiles - 1)),
            dma((count // block + 1, tiles - 1)),
            dma,
            dma((spans + 1, tiles - 1)),
            dma((spans + 1, tiles - 1)),
            dma((spans,)),
            dma((spans,)),
            dma((spans,)),
            dma((2,)),
            dma((n_one,)),
        ],
        compiler_params=pltpu.CompilerParams(
            collective_id=0, has_side_effects=True, vmem_limit_bytes=63 << 20
        ),
    )(
        raw_echo,
        phase_scaling,
        phase_range,
        phase_azimuth,
        left_table(rows, np.arange(q), m, -1),
        twist_table(4, m, extent, 1),
        right_table(lane, lane, LANES, -1),
        right_table(lane, lane, LANES, 1, 1.0 / ranges),
        np.stack([c, s]).astype(np.float32),
        left_table(rows, rows, m, 1, 1.0 / extent),
    )


def solution(mesh):
    return jax.shard_map(
        body,
        mesh=mesh,
        in_specs=(
            P(None, ("strip", "az", "tile"), None),
            P(None, "tile"),
            P("tile", None),
            P(None, "tile"),
        ),
        out_specs=P(None, ("strip", "az"), "tile"),
        check_vma=False,
    )
```

profile of v0, /device:TPU:16, one launch (start us, length us, event | category | flops | bytes accessed | tf_op | source)
XLA Modules:
  0.0 254.2 jit_solution(15574470003760717154)
XLA Ops:
  0.0 249.4 %shard_map.100 = f32[2,512,1024]{2,1,0:T(8,128)} custom-call(f32[2,128,4096]{2,1,0:T(8,128)} %raw_ref.1, f32[1024,1024]{1,0:T(8,128)} %scaling_ref.1, f32[256,4096]{1,0:T(8,128)} %range_ref.1, f32[1024,1024]{1,0:T(8,128)} %azimuth_ref.1, bf16[2,512,256]{2,1,0:T(8,128)(2,1)} %constant.12.clone.front_ref, f32[2,4,256,128]{3,2,1,0:T(8,128)} %constant.13.clone.twist_ref, ...), custom_call_target="tpu_custom_call" | custom-call | tf_op jit(solution)/shard_map/pallas_call | solution.py:511
  249.4 4.8 %copy.12 = f32[2,512,1024]{2,1,0:T(8,128)} copy(f32[2,512,1024]{2,1,0:T(8,128)} %shard_map.100) | data formatting | bytes 8388608
where the time goes:
time: 257 us; the launch traced here: 254 us
  Pallas kernels  249 us (97%)
  local copies, waits for them, and re-layouts  4.79 us (2%)
    pallas_call x1, Pallas kernels, body(): pl.pallas_call(functools.partial(focus_kernel, tiles, length, block), out...  249 us

commit v1 on v0

--- a/solution.py
+++ b/solution.py
@@ -494,7 +494,7 @@
             onward(j).wait_send()
 
 
-def body(raw_echo, phase_scaling, phase_range, phase_azimuth):
+def tail_body(raw_echo, phase_scaling, phase_range, phase_azimuth):
     tiles = lax.axis_size("tile")
     length = lax.axis_size("az")
     pulses = raw_echo.shape[1] * tiles
@@ -557,6 +557,572 @@
     )
 
 
+def pair_rows(extent, chip, core):
+    m = extent // 4
+    return 2 * np.arange(m // 2) + chip + m * core
+
+
+def pair_front(extent, pulses, tiles):
+    out = []
+    for t in range(tiles):
+        rows = pair_rows(extent, t // 2, t % 2)
+        out.append(np.stack([left_table(rows, 2 * np.arange(pulses // 2) + e, extent, -1) for e in (0, 1)], axis=1))
+    return np.stack(out)
+
+
+def filter_block(
+    x_ref, base, block, scal_ref, fwd_ref, inv_ref, twist_ref, phase_ref, hi_ref, lo_ref, mid_ref
+):
+    n_one = phase_ref.shape[0]
+    step = 16
+    group = max(1, 256 // block)
+    f_hi, f_lo = fwd_ref[0], fwd_ref[1]
+    b_hi, b_lo = inv_ref[0], inv_ref[1]
+    whole = pl.ds(pl.multiple_of(base, block), block)
+
+    @pl.loop(0, n_one)
+    def _(a):
+        x = times((x_ref[0, whole, lanes(a)], x_ref[1, whole, lanes(a)]), sincos(scal_ref[whole, lanes(a)]))
+        x_ref[0, whole, lanes(a)] = x[0]
+        x_ref[1, whole, lanes(a)] = x[1]
+
+    @pl.loop(0, block // step)
+    def _(i):
+        rows = pl.ds(pl.multiple_of(i * step, step), step)
+        at = pl.ds(pl.multiple_of(base + i * step, step), step)
+        v = [
+            tuple(x_ref[c, at, pl.ds(a * LANES, LANES)] for c in (0, 1))
+            for a in range(n_one)
+        ]
+        for k, x in enumerate(fft(v, -1)):
+            if k:
+                x = times(x, (twist_ref[0, k : k + 1, :], twist_ref[1, k : k + 1, :]))
+            for c in (0, 1):
+                h, l = split(x[c])
+                hi_ref[k, rows, pl.ds(c * LANES, LANES)] = h
+                lo_ref[k, rows, pl.ds(c * LANES, LANES)] = l
+
+    @pl.loop(0, n_one // group)
+    def _(i):
+        ks = pl.ds(i * group, group)
+        flat = (group * block, 2 * LANES)
+        h, l = hi_ref[ks].reshape(flat), lo_ref[ks].reshape(flat)
+        r = mm(h, f_hi) + mm(l, f_hi) + mm(h, f_lo)
+        turn = phase_ref[ks, whole, :]
+        r = times((r[:, :LANES], r[:, LANES:]), sincos(turn.reshape(group * block, LANES)))
+        h, l = split(jnp.concatenate(r, axis=1))
+        r = mm(h, b_hi) + mm(l, b_hi) + mm(h, b_lo)
+        at = pl.ds(pl.multiple_of(i * group * block, block), group * block)
+        mid_ref[0, at, :] = r[:, :LANES]
+        mid_ref[1, at, :] = r[:, LANES:]
+
+    @pl.loop(0, block // 8)
+    def _(i):
+        at = pl.ds(pl.multiple_of(base + i * 8, 8), 8)
+        v = []
+        for k in range(n_one):
+            x = tuple(mid_ref[c, pl.ds(pl.multiple_of(k * block + i * 8, 8), 8), :] for c in (0, 1))
+            if k:
+                x = times(x, (twist_ref[0, k : k + 1, :], -twist_ref[1, k : k + 1, :]))
+            v.append(x)
+        for a, x in enumerate(fft(v, 1)):
+            for c in (0, 1):
+                x_ref[c, at, pl.ds(a * LANES, LANES)] = x[c]
+
+
+def turn_rows(load, mid, turn, base):
+    n_one = turn.shape[0]
+    half = n_one * LANES // 2
+    part = half // n_one
+    per = half // LANES
+    at = pl.ds(pl.multiple_of(base, LANES), LANES)
+
+    @pl.loop(0, n_one)
+    def _(g):
+        mid[g // per, pl.ds(pl.multiple_of(g % per * LANES, LANES), LANES), :] = load(g).T
+
+    @pl.loop(0, n_one)
+    def _(k):
+        rows = pl.ds(k, part, stride=n_one)
+        x = jnp.concatenate([mid[h, rows, :] for h in range(LANES // part)], axis=0)
+        turn[k, at, :] = x.T
+
+
+def pair_kernel(
+    n_strip, n_az, block, chunk,
+    raw_ref, scaling_ref, range_ref, azimuth_ref, front_ref,
+    twist_ref, fwd_ref, inv_ref, range_twist_ref, table_ref,
+    o_ref,
+    cols, prev, dop, scal, far, turn, phase, ret, for_core, for_chip, for_range,
+    front, head, hi_ref, lo_ref, mid,
+    load, load_range, load_echo, load_front, z_send, z_recv, y_send, y_recv, c_send, c_recv, f_send, f_recv,
+    s_send, s_recv, p_send, p_recv, az_send, az_recv, x_send, x_recv,
+    w_send, w_recv, w_local, v_send, v_recv, v_local, out_sem,
+):
+    t = lax.axis_index("tile")
+    az = lax.axis_index("az")
+    strip = lax.axis_index("strip")
+    y, c = t // 2, t % 2
+    tiles = 4
+    count, ranges = range_ref.shape
+    half = count // 2
+    extent, width = scaling_ref.shape
+    m = extent // 4
+    pulses = o_ref.shape[1]
+    q = pulses // 4
+    rows_own = raw_ref.shape[1]
+    spans = width // LANES
+    n_one = ranges // LANES
+    chunks = n_one // chunk
+    blocks = count // block
+    part = half // blocks
+    whole = blocks // 2 + 1
+    partner, across = {"tile": 2 * y + 1 - c}, {"tile": 2 * (1 - y) + c}
+    other = pl.ds(pl.multiple_of(2 * (1 - y) * width, LANES), 2 * width)
+    mine = pl.ds(pl.multiple_of(t * width, LANES), width)
+    slab = strip * n_az + az
+
+    def remote(src, dst, send, recv, device):
+        return pltpu.make_async_remote_copy(
+            src_ref=src, dst_ref=dst, send_sem=send, recv_sem=recv,
+            device_id=device, device_id_type=pl.DeviceIdType.MESH,
+        )
+
+    def pulse_rows(tile):
+        return pl.ds(pl.multiple_of(tile * rows_own, rows_own), rows_own)
+
+    def groups(j):
+        return pl.ds(j * chunk, chunk)
+
+    def onward(a):
+        return remote(
+            raw_ref.at[:, :, lanes(a)], prev.at[a], z_send.at[a], z_recv.at[a],
+            {"az": lax.rem(az + 1, n_az)},
+        )
+
+    def own_echo(a):
+        return pltpu.make_async_copy(
+            raw_ref.at[:, :, lanes(a)], cols.at[a, :, pulse_rows(t), :], load_echo.at[a]
+        )
+
+    def own_range(a):
+        return pltpu.make_async_copy(range_ref.at[:, lanes(a)], turn.at[a], load_range.at[a])
+
+    def own_phase(source, j, k):
+        return pltpu.make_async_copy(source.at[:, lanes(j)], phase.at[j], load.at[k, j])
+
+    def echo_across(j):
+        return remote(
+            prev.at[groups(j)], cols.at[groups(j), :, pulse_rows(t), :],
+            y_send.at[j], y_recv.at[j], across,
+        )
+
+    def echo_core(j):
+        at = cols.at[groups(j), :, pulse_rows(t), :]
+        return remote(at, at, c_send.at[j], c_recv.at[j], partner)
+
+    def echo_forward(j):
+        at = cols.at[groups(j), :, pulse_rows(2 * (1 - y) + c), :]
+        return remote(at, at, f_send.at[j], f_recv.at[j], partner)
+
+    def scaling_core():
+        return remote(for_core, scal.at[:, mine], s_send, s_recv, partner)
+
+    def scaling_chip(k):
+        to = {"tile": 2 * (1 - y) + lax.rem(c + k, 2)}
+        return remote(
+            for_chip.at[lax.rem(c + k, 2)],
+            scal.at[pl.ds(pl.multiple_of(slab * block, block), block), mine],
+            p_send.at[k], p_recv.at[k], to,
+        )
+
+    def far_rows(g):
+        return far.at[pl.ds(pl.multiple_of(g * part, part), part), :]
+
+    def scal_rows(g):
+        return scal.at[pl.ds(pl.multiple_of(g * block, block), block), other]
+
+    def range_chip():
+        return remote(for_range, far_rows(slab), p_send.at[2], p_recv.at[2], across)
+
+    def along(d, z, k):
+        to = {"az": lax.rem(az + d, n_az)}
+        at = (scal_rows, far_rows)[k](strip * n_az + z)
+        return remote(at, at, az_send.at[d, k], az_recv.at[z, k], to)
+
+    def sideways(z, k):
+        at = (scal_rows, far_rows)[k](strip * n_az + z)
+        return remote(at, at, x_send.at[z, k], x_recv.at[z, k], {"strip": 1 - strip})
+
+    def order(n):
+        return jnp.where(az + n < n_az, az + n, n_az - 1 - n)
+
+    def place(n):
+        s = y if n < n_az else 1 - y
+        z = order(n % n_az)
+        base = (s * n_az + z) * block
+        row = (2 * s + c) * m + y * half + z * block
+        return pl.ds(pl.multiple_of(base, block), block), pl.ds(pl.multiple_of(row, block), block), base
+
+    def back(n, k):
+        to = lax.rem(t + k, tiles)
+        src, dst, _ = place(n)
+        at = pl.ds(pl.multiple_of(to * width, LANES), width)
+        return remote(
+            dop.at[:, src, at], ret.at[:, dst, :], w_send.at[n, k - 1], w_recv.at[n, k - 1], {"tile": to}
+        )
+
+    def keep(n):
+        src, dst, _ = place(n)
+        return pltpu.make_async_copy(dop.at[:, src, mine], ret.at[:, dst, :], w_local.at[n])
+
+    def back_span(j, n, k):
+        to = lax.rem(t + k, tiles)
+        src, dst, _ = place(n)
+        return remote(
+            dop.at[:, src, lanes(to * spans + j)], ret.at[:, dst, lanes(j)],
+            v_send.at[j, n - whole, k - 1], v_recv.at[j, n - whole, k - 1], {"tile": to},
+        )
+
+    def keep_span(j, n):
+        src, dst, _ = place(n)
+        return pltpu.make_async_copy(
+            dop.at[:, src, lanes(t * spans + j)], ret.at[:, dst, lanes(j)], v_local.at[j, n - whole]
+        )
+
+    def put(j):
+        slot = lax.rem(j, 2)
+        return pltpu.make_async_copy(head.at[slot], o_ref.at[:, :, lanes(j)], out_sem.at[slot])
+
+    get_front = pltpu.make_async_copy(front_ref.at[t], front, load_front)
+
+    @pl.loop(0, spans)
+    def _(j):
+        own_phase(scaling_ref, j, 0).start()
+
+    @pl.loop(0, n_one)
+    def _(a):
+        own_range(a).start()
+
+    @pl.loop(0, n_one)
+    def _(a):
+        own_echo(a).start()
+
+    get_front.start()
+    barrier = greet(
+        [{"tile": lax.rem(t + k, tiles)} for k in range(1, tiles)]
+        + [{"az": lax.rem(az + k, n_az)} for k in range(1, n_az)]
+        + [{"strip": 1 - strip}]
+    )
+    pl.semaphore_wait(barrier, tiles + n_az - 1)
+
+    @pl.when(az < n_az - 1)
+    def _():
+        @pl.loop(0, n_one)
+        def _(a):
+            onward(a).start()
+
+    @pl.when(az == 0)
+    def _():
+        @pl.loop(0, n_one)
+        def _(a):
+            prev[a] = jnp.zeros((2, rows_own, LANES), F32)
+
+    @pl.loop(0, spans)
+    def _(j):
+        own_phase(scaling_ref, j, 0).wait()
+        for k in (0, 1):
+            first = (2 * strip + k) * m + 2 * az * block + 1 - y
+            for_chip[k, :, lanes(j)] = phase[j, pl.ds(first, block, stride=2), :]
+
+    for k in (0, 1):
+        scaling_chip(k).start()
+
+    @pl.loop(0, n_one)
+    def _(g):
+        own_range(g).wait()
+        for_range[:, lanes(g)] = turn[g, pl.ds(2 * part * slab + 1 - y, part, stride=2), :]
+
+    range_chip().start()
+
+    @pl.loop(0, spans)
+    def _(j):
+        for h in (0, 1):
+            rows = pl.ds(h * half, half)
+            for_core[rows, lanes(j)] = phase[j, pl.ds((2 * h + 1 - c) * m + y, half, stride=2), :]
+            scal[rows, lanes(t * spans + j)] = phase[j, pl.ds((2 * h + c) * m + y, half, stride=2), :]
+
+    scaling_core().start()
+    turn_rows(lambda g: turn[g, pl.ds(y, half, stride=2), :], mid, turn, y * half)
+
+    @pl.loop(0, spans)
+    def _(j):
+        own_phase(azimuth_ref, j, 1).start()
+
+    get_front.wait()
+    sign = (1 - 2 * y).astype(F32)
+
+    @pl.loop(0, chunks + 3)
+    def _(j):
+        @pl.when(j < chunks)
+        def _():
+            for i in range(chunk):
+                at = j * chunk + i
+                own_echo(at).wait()
+
+                @pl.when(az > 0)
+                def _():
+                    onward(at).wait_recv()
+
+                for k in (0, 1):
+                    a = cols[at, k, pulse_rows(t), :]
+                    b = prev[at, k] * sign
+                    cols[at, k, pulse_rows(t), :] = a + b
+                    prev[at, k] = a - b
+            echo_across(j).start()
+            echo_core(j).start()
+
+        @pl.when(j == 4)
+        def _():
+            for k in (0, 1):
+                scaling_chip(k).wait_recv()
+            range_chip().wait_recv()
+            for k in (0, 1):
+                sideways(az, k).start()
+                for d in range(n_az - 1, 0, -1):
+                    along(d, az, k).start()
+
+        for d in range(1, n_az):
+            @pl.when((j == chunks - n_az + d - 1) & (az + d < n_az))
+            def _():
+                for k in (0, 1):
+                    along(n_az - d, az + d, k).wait_recv()
+                    sideways(az + d, k).start()
+
+        @pl.when((j >= 2) & (j < chunks + 2))
+        def _():
+            echo_across(j - 2).wait_recv()
+            echo_forward(j - 2).start()
+
+        @pl.when(j >= 3)
+        def _():
+            now = j - 3
+            echo_core(now).wait_recv()
+            echo_forward(now).wait_recv()
+            r = []
+            for e in (0, 1):
+                rows = pl.ds(e, pulses // 2, stride=2)
+                s = jnp.concatenate(
+                    [
+                        jnp.concatenate([cols[now * chunk + i, k, rows, :] for k in (0, 1)], axis=0)
+                        for i in range(chunk)
+                    ],
+                    axis=1,
+                )
+                s_hi, s_lo = split(s)
+                hi, lo = front[0, e], front[1, e]
+                r.append(mm(hi, s_hi) + mm(hi, s_lo) + mm(lo, s_hi))
+            for k in (0, 1):
+                a, b = (x[k * half : (k + 1) * half] for x in r)
+                at = pl.ds(pl.multiple_of(now * chunk * LANES, LANES), chunk * LANES)
+                dop[k, pl.ds(0, half), at] = a + b
+                dop[k, pl.ds(half, half), at] = a - b
+
+    scaling_core().wait_recv()
+
+    for n in range(blocks):
+        if n < n_az:
+            z = order(n)
+
+            @pl.when(az + n >= n_az)
+            def _():
+                for k in (0, 1):
+                    along(n_az - 1, z, k).wait_recv()
+                    sideways(z, k).start()
+
+            for k in (0, 1):
+                sideways(z, k).wait_recv()
+        if n == n_az:
+            turn_rows(lambda g: far[:, lanes(g)], mid, turn, (1 - y) * half)
+        filter_block(
+            dop, place(n)[2], block, scal, fwd_ref, inv_ref, range_twist_ref, turn, hi_ref, lo_ref, mid
+        )
+        if n < whole:
+            for k in range(tiles - 1, 0, -1):
+                back(n, k).start()
+            keep(n).start()
+
+    @pl.loop(0, spans)
+    def _(j):
+        for n in range(whole, blocks):
+            for k in range(tiles - 1, 0, -1):
+                back_span(j, n, k).start()
+            keep_span(j, n).start()
+
+    @pl.loop(0, spans)
+    def _(j):
+        own_phase(azimuth_ref, j, 1).wait()
+
+    for n in range(whole):
+        for k in range(1, tiles):
+            back(n, k).wait_recv()
+        keep(n).wait()
+
+    @pl.loop(0, spans)
+    def _(j):
+        for n in range(whole, blocks):
+            for k in range(1, tiles):
+                back_span(j, n, k).wait_recv()
+            keep_span(j, n).wait()
+        hi, lo = table_ref[0], table_ref[1]
+        slot = lax.rem(j, 2)
+
+        @pl.when(j > 1)
+        def _():
+            put(j - 2).wait()
+
+        v = []
+        for f in range(4):
+            rows = pl.ds(f * m, m)
+            angle = jnp.concatenate(
+                [phase[j, pl.ds(f * m + p, half, stride=2), :] for p in (0, 1)], axis=0
+            )
+            v.append(times((ret[0, rows, lanes(j)], ret[1, rows, lanes(j)]), sincos(angle)))
+        for e, x in enumerate(four(v, 1)):
+            if e:
+                x = times(x, (twist_ref[0, e], twist_ref[1, e]))
+            s_hi, s_lo = split(jnp.concatenate(x, axis=0))
+            r = mm(hi, s_hi) + mm(hi, s_lo) + mm(lo, s_hi)
+            for k in (0, 1):
+                head[slot, k, pl.ds(e, q, stride=4), :] = r[k * q : (k + 1) * q]
+        put(j).start()
+
+    for j in range(max(0, spans - 2), spans):
+        put(j).wait()
+
+    @pl.when(az < n_az - 1)
+    def _():
+        @pl.loop(0, n_one)
+        def _(a):
+            onward(a).wait_send()
+
+    @pl.loop(0, chunks)
+    def _(j):
+        echo_across(j).wait_send()
+        echo_core(j).wait_send()
+        echo_forward(j).wait_send()
+
+    scaling_core().wait_send()
+    range_chip().wait_send()
+    for k in (0, 1):
+        scaling_chip(k).wait_send()
+        for d in range(1, n_az):
+            along(d, az, k).wait_send()
+        for z in range(n_az):
+            sideways(z, k).wait_send()
+    for n in range(whole):
+        for k in range(1, tiles):
+            back(n, k).wait_send()
+
+    @pl.loop(0, spans)
+    def _(j):
+        for n in range(whole, blocks):
+            for k in range(1, tiles):
+                back_span(j, n, k).wait_send()
+
+
+def pair_body(raw_echo, phase_scaling, phase_range, phase_azimuth):
+    tiles = lax.axis_size("tile")
+    n_az, n_strip = lax.axis_size("az"), lax.axis_size("strip")
+    pulses = raw_echo.shape[1] * tiles
+    extent, width = phase_scaling.shape
+    count, ranges = phase_range.shape
+    m, q, half = extent // 4, pulses // 4, count // 2
+    n_one, spans = ranges // LANES, width // LANES
+    blocks = n_strip * n_az
+    block = count // blocks
+    chunk = 2
+    chunks = n_one // chunk
+    whole = blocks // 2 + 1
+    rest = blocks - whole
+    fine = np.concatenate([np.arange(0, m, 2), np.arange(1, m, 2)])
+    lane = np.arange(LANES)
+    vmem = pl.BlockSpec(memory_space=pltpu.VMEM)
+    anyspace = pl.BlockSpec(memory_space=pl.ANY)
+    dma = pltpu.SemaphoreType.DMA
+    c, s = roots(np.arange(n_one), lane, ranges, -1)
+    return pl.pallas_call(
+        functools.partial(pair_kernel, n_strip, n_az, block, chunk),
+        out_shape=jax.ShapeDtypeStruct((2, pulses, width), F32),
+        in_specs=[anyspace] * 5 + [vmem] * 5,
+        out_specs=anyspace,
+        scratch_shapes=[
+            pltpu.VMEM((n_one, 2, pulses, LANES), F32),
+            pltpu.VMEM((n_one, 2, pulses // tiles, LANES), F32),
+            pltpu.VMEM((2, count, ranges), F32),
+            pltpu.VMEM((count, ranges), F32),
+            pltpu.VMEM((half, ranges), F32),
+            pltpu.VMEM((n_one, count, LANES), F32),
+            pltpu.VMEM((spans, extent, LANES), F32),
+            pltpu.VMEM((2, extent, width), F32),
+            pltpu.VMEM((count, width), F32),
+            pltpu.VMEM((2, block, width), F32),
+            pltpu.VMEM((half // blocks, ranges), F32),
+            pltpu.VMEM((2, 2, count, pulses), BF16),
+            pltpu.VMEM((2, 2, pulses, LANES), F32),
+            pltpu.VMEM((n_one, block, 2 * LANES), BF16),
+            pltpu.VMEM((n_one, block, 2 * LANES), BF16),
+            pltpu.VMEM((2, n_one * LANES // 2, LANES), F32),
+            dma((2, spans)), dma((n_one,)), dma((n_one,)), dma,
+            dma((n_one,)), dma((n_one,)),
+            dma((chunks,)), dma((chunks,)),
+            dma((chunks,)), dma((chunks,)),
+            dma((chunks,)), dma((chunks,)),
+            dma, dma,
+            dma((3,)), dma((3,)),
+            dma((n_az, 2)), dma((n_az, 2)),
+            dma((n_az, 2)), dma((n_az, 2)),
+            dma((whole, tiles - 1)), dma((whole, tiles - 1)), dma((whole,)),
+            dma((spans, rest, tiles - 1)), dma((spans, rest, tiles - 1)), dma((spans, rest)),
+            dma((2,)),
+        ],
+        compiler_params=pltpu.CompilerParams(
+            collective_id=0, has_side_effects=True, vmem_limit_bytes=63 << 20
+        ),
+    )(
+        raw_echo,
+        phase_scaling,
+        phase_range,
+        phase_azimuth,
+        pair_front(extent, pulses, tiles),
+        np.ascontiguousarray(twist_table(4, m, extent, 1)[:, :, fine]),
+        right_table(lane, lane, LANES, -1),
+        right_table(lane, lane, LANES, 1, 1.0 / ranges),
+        np.stack([c, s]).astype(np.float32),
+        left_table(np.arange(q), fine, m, 1, 1.0 / extent),
+    )
+
+
+def paired(raw_echo, phase_scaling, phase_range):
+    tiles, n_az, n_strip = (lax.axis_size(a) for a in ("tile", "az", "strip"))
+    count = phase_range.shape[0]
+    blocks = n_az * n_strip
+    return (
+        tiles == 4
+        and n_strip == 2
+        and n_az > 1
+        and count == 2 * LANES
+        and phase_scaling.shape[0] == 2 * raw_echo.shape[1] * tiles
+        and count % (16 * blocks) == 0
+        and phase_range.shape[1] % (2 * LANES) == 0
+    )
+
+
+def body(raw_echo, phase_scaling, phase_range, phase_azimuth):
+    plan = pair_body if paired(raw_echo, phase_scaling, phase_range) else tail_body
+    return plan(raw_echo, phase_scaling, phase_range, phase_azimuth)
+
+
 def solution(mesh):
     return jax.shard_map(
         body,

time: 257 us -> 240 us (0.934)
  Pallas kernels: 249 us -> 235 us
    pallas_call x1, Pallas kernels: 249 us -> 235 us  [pair_body(): pl.pallas_call(functools.partial(pair_kernel, n_strip, n_az, block, chunk...]
where the time goes in v1:
time: 240 us
  Pallas kernels  235 us (98%)
  local copies, waits for them, and re-layouts  4.79 us (2%)
    pallas_call x1, Pallas kernels, pair_body(): pl.pallas_call(functools.partial(pair_kernel, n_strip, n_az, block, chunk...  235 us

profile of v1, /device:TPU:16, one launch (start us, length us, event | category | flops | bytes accessed | tf_op | source)
XLA Modules:
  0.0 239.6 jit_solution(15320431184919738985)
XLA Ops:
  0.0 234.8 %shard_map.100 = f32[2,512,1024]{2,1,0:T(8,128)} custom-call(f32[2,128,4096]{2,1,0:T(8,128)} %raw_ref.1, f32[1024,1024]{1,0:T(8,128)} %scaling_ref.1, f32[256,4096]{1,0:T(8,128)} %range_ref.1, f32[1024,1024]{1,0:T(8,128)} %azimuth_ref.1, bf16[4,2,2,256,512]{4,3,2,1,0:T(8,128)(2,1)} %constant.12.clone.front_ref, f32[2,4,256,128]{3,2,1,0:T(8,128)} %constant.13.clone.twist_ref, ...), custom_call_target="tpu_custom_call" | custom-call | tf_op jit(solution)/shard_map/pallas_call | solution.py:1054
  234.9 4.8 %copy.12 = f32[2,512,1024]{2,1,0:T(8,128)} copy(f32[2,512,1024]{2,1,0:T(8,128)} %shard_map.100) | data formatting | bytes 8388608

commit v2 on v1

--- a/solution.py
+++ b/solution.py
@@ -557,17 +557,23 @@
     )
 
 
-def pair_rows(extent, chip, core):
+def pair_front(extent, pulses):
     m = extent // 4
-    return 2 * np.arange(m // 2) + chip + m * core
-
-
-def pair_front(extent, pulses, tiles):
-    out = []
-    for t in range(tiles):
-        rows = pair_rows(extent, t // 2, t % 2)
-        out.append(np.stack([left_table(rows, 2 * np.arange(pulses // 2) + e, extent, -1) for e in (0, 1)], axis=1))
-    return np.stack(out)
+    return np.stack(
+        [left_table(2 * np.arange(m // 2) + y, 2 * np.arange(pulses // 2), extent, -1) for y in (0, 1)]
+    )
+
+
+def pair_twists(extent, fine):
+    m = extent // 4
+    out = np.zeros((m, LANES), np.float32)
+    for e in range(1, 4):
+        c, s = roots(fine, [e], extent, 1)
+        out[:, 2 * e - 2 : 2 * e - 1], out[:, 2 * e - 1 : 2 * e] = c, s
+    for t in range(4):
+        c, s = roots(2 * np.arange(m // 2) + t // 2 + m * (t % 2), [1], extent, -1)
+        out[: m // 2, 6 + 2 * t : 7 + 2 * t], out[: m // 2, 7 + 2 * t : 8 + 2 * t] = c, s
+    return out
 
 
 def filter_block(
@@ -651,10 +657,10 @@
 def pair_kernel(
     n_strip, n_az, block, chunk,
     raw_ref, scaling_ref, range_ref, azimuth_ref, front_ref,
-    twist_ref, fwd_ref, inv_ref, range_twist_ref, table_ref,
+    twists_ref, fwd_ref, inv_ref, range_twist_ref, table_ref,
     o_ref,
     cols, prev, dop, scal, far, turn, phase, ret, for_core, for_chip, for_range,
-    front, head, hi_ref, lo_ref, mid,
+    front, turn_front, twist_ref, head, hi_ref, lo_ref, mid,
     load, load_range, load_echo, load_front, z_send, z_recv, y_send, y_recv, c_send, c_recv, f_send, f_recv,
     s_send, s_recv, p_send, p_recv, az_send, az_recv, x_send, x_recv,
     w_send, w_recv, w_local, v_send, v_recv, v_local, out_sem,
@@ -758,8 +764,8 @@
         return jnp.where(az + n < n_az, az + n, n_az - 1 - n)
 
     def place(n):
-        s = y if n < n_az else 1 - y
-        z = order(n % n_az)
+        s = jnp.where(n < n_az, y, 1 - y)
+        z = order(lax.rem(n, n_az))
         base = (s * n_az + z) * block
         row = (2 * s + c) * m + y * half + z * block
         return pl.ds(pl.multiple_of(base, block), block), pl.ds(pl.multiple_of(row, block), block), base
@@ -794,7 +800,7 @@
         slot = lax.rem(j, 2)
         return pltpu.make_async_copy(head.at[slot], o_ref.at[:, :, lanes(j)], out_sem.at[slot])
 
-    get_front = pltpu.make_async_copy(front_ref.at[t], front, load_front)
+    get_front = pltpu.make_async_copy(front_ref.at[y], front, load_front)
 
     @pl.loop(0, spans)
     def _(j):
@@ -859,7 +865,17 @@
     def _(j):
         own_phase(azimuth_ref, j, 1).start()
 
+    for k in range(6):
+        twist_ref[k] = jnp.broadcast_to(twists_ref[:, k : k + 1], (m, LANES))
+    for k in (0, 1):
+        x = twists_ref[pl.ds(0, half), 6 + k : 7 + k]
+        for i in range(1, tiles):
+            x = jnp.where(t == i, twists_ref[pl.ds(0, half), 6 + 2 * i + k : 7 + 2 * i + k], x)
+        turn_front[k] = jnp.broadcast_to(x, (half, LANES))
     get_front.wait()
+    odd = lax.rem(lax.broadcasted_iota(jnp.int32, (1, pulses), 1), 2) * c
+    for k in (0, 1):
+        front[k] = (front[k].astype(F32) * (1 - 2 * odd).astype(F32)).astype(BF16)
     sign = (1 - 2 * y).astype(F32)
 
     @pl.loop(0, chunks + 3)
@@ -920,18 +936,23 @@
                     axis=1,
                 )
                 s_hi, s_lo = split(s)
-                hi, lo = front[0, e], front[1, e]
-                r.append(mm(hi, s_hi) + mm(hi, s_lo) + mm(lo, s_hi))
+                hi, lo = front[0], front[1]
+                x = mm(hi, s_hi) + mm(hi, s_lo) + mm(lo, s_hi)
+                r.append((x[:half], x[half:]))
+            w = tuple(jnp.concatenate([turn_front[k]] * chunk, axis=1) for k in (0, 1))
+            r[1] = times(r[1], w)
             for k in (0, 1):
-                a, b = (x[k * half : (k + 1) * half] for x in r)
+                a, b = r[0][k], r[1][k]
                 at = pl.ds(pl.multiple_of(now * chunk * LANES, LANES), chunk * LANES)
                 dop[k, pl.ds(0, half), at] = a + b
                 dop[k, pl.ds(half, half), at] = a - b
 
     scaling_core().wait_recv()
 
-    for n in range(blocks):
-        if n < n_az:
+    @pl.loop(0, blocks)
+    def _(n):
+        @pl.when(n < n_az)
+        def _():
             z = order(n)
 
             @pl.when(az + n >= n_az)
@@ -942,12 +963,17 @@
 
             for k in (0, 1):
                 sideways(z, k).wait_recv()
-        if n == n_az:
+
+        @pl.when(n == n_az)
+        def _():
             turn_rows(lambda g: far[:, lanes(g)], mid, turn, (1 - y) * half)
+
         filter_block(
             dop, place(n)[2], block, scal, fwd_ref, inv_ref, range_twist_ref, turn, hi_ref, lo_ref, mid
         )
-        if n < whole:
+
+        @pl.when(n < whole)
+        def _():
             for k in range(tiles - 1, 0, -1):
                 back(n, k).start()
             keep(n).start()
@@ -990,7 +1016,7 @@
             v.append(times((ret[0, rows, lanes(j)], ret[1, rows, lanes(j)]), sincos(angle)))
         for e, x in enumerate(four(v, 1)):
             if e:
-                x = times(x, (twist_ref[0, e], twist_ref[1, e]))
+                x = times(x, (twist_ref[2 * e - 2], twist_ref[2 * e - 1]))
             s_hi, s_lo = split(jnp.concatenate(x, axis=0))
             r = mm(hi, s_hi) + mm(hi, s_lo) + mm(lo, s_hi)
             for k in (0, 1):
@@ -1068,7 +1094,9 @@
             pltpu.VMEM((count, width), F32),
             pltpu.VMEM((2, block, width), F32),
             pltpu.VMEM((half // blocks, ranges), F32),
-            pltpu.VMEM((2, 2, count, pulses), BF16),
+            pltpu.VMEM((2, count, pulses), BF16),
+            pltpu.VMEM((2, half, LANES), F32),
+            pltpu.VMEM((6, m, LANES), F32),
             pltpu.VMEM((2, 2, pulses, LANES), F32),
             pltpu.VMEM((n_one, block, 2 * LANES), BF16),
             pltpu.VMEM((n_one, block, 2 * LANES), BF16),
@@ -1094,8 +1122,8 @@
         phase_scaling,
         phase_range,
         phase_azimuth,
-        pair_front(extent, pulses, tiles),
-        np.ascontiguousarray(twist_table(4, m, extent, 1)[:, :, fine]),
+        pair_front(extent, pulses),
+        pair_twists(extent, fine),
         right_table(lane, lane, LANES, -1),
         right_table(lane, lane, LANES, 1, 1.0 / ranges),
         np.stack([c, s]).astype(np.float32),

time: 240 us -> 240 us (level)
  no operation moved by 1% of the time
where the time goes in v2:
time: 240 us
  Pallas kernels  235 us (98%)
  local copies, waits for them, and re-layouts  4.79 us (2%)
    pallas_call x1, Pallas kernels, pair_body(): pl.pallas_call(functools.partial(pair_kernel, n_strip, n_az, block, chunk...  235 us

profile of v2, /device:TPU:16, one launch (start us, length us, event | category | flops | bytes accessed | tf_op | source)
XLA Modules:
  0.0 239.5 jit_solution(10564553092656606852)
XLA Ops:
  0.0 234.7 %shard_map.100 = f32[2,512,1024]{2,1,0:T(8,128)} custom-call(f32[2,128,4096]{2,1,0:T(8,128)} %raw_ref.1, f32[1024,1024]{1,0:T(8,128)} %scaling_ref.1, f32[256,4096]{1,0:T(8,128)} %range_ref.1, f32[1024,1024]{1,0:T(8,128)} %azimuth_ref.1, bf16[2,2,256,512]{3,2,1,0:T(8,128)(2,1)} %constant.12.clone.front_ref, f32[256,128]{1,0:T(8,128)} %constant.13.clone.twists_ref, ...), custom_call_target="tpu_custom_call" | custom-call | tf_op jit(solution)/shard_map/pallas_call | solution.py:1080
  234.7 4.8 %copy.12 = f32[2,512,1024]{2,1,0:T(8,128)} copy(f32[2,512,1024]{2,1,0:T(8,128)} %shard_map.100) | data formatting | bytes 8388608

commit v3 on v2

--- a/solution.py
+++ b/solution.py
@@ -659,10 +659,10 @@
     raw_ref, scaling_ref, range_ref, azimuth_ref, front_ref,
     twists_ref, fwd_ref, inv_ref, range_twist_ref, table_ref,
     o_ref,
-    cols, prev, dop, scal, far, turn, phase, ret, for_core, for_chip, for_range,
+    cols, prev, dop, scal, swap, turn, phase, ret, for_chip,
     front, turn_front, twist_ref, head, hi_ref, lo_ref, mid,
     load, load_range, load_echo, load_front, z_send, z_recv, y_send, y_recv, c_send, c_recv, f_send, f_recv,
-    s_send, s_recv, p_send, p_recv, az_send, az_recv, x_send, x_recv,
+    s_send, s_recv, p_send, p_recv, az_send, up_send, az_recv, x_send, x_recv,
     w_send, w_recv, w_local, v_send, v_recv, v_local, out_sem,
 ):
     t = lax.axis_index("tile")
@@ -711,8 +711,12 @@
             raw_ref.at[:, :, lanes(a)], cols.at[a, :, pulse_rows(t), :], load_echo.at[a]
         )
 
+    def range_piece(a, first, rows, stride=None):
+        row = a % (extent // count) * count + first
+        return phase.at[a // (extent // count), pl.ds(row, rows, stride=stride), :]
+
     def own_range(a):
-        return pltpu.make_async_copy(range_ref.at[:, lanes(a)], turn.at[a], load_range.at[a])
+        return pltpu.make_async_copy(range_ref.at[:, lanes(a)], range_piece(a, 0, count), load_range.at[a])
 
     def own_phase(source, j, k):
         return pltpu.make_async_copy(source.at[:, lanes(j)], phase.at[j], load.at[k, j])
@@ -732,7 +736,7 @@
         return remote(at, at, f_send.at[j], f_recv.at[j], partner)
 
     def scaling_core():
-        return remote(for_core, scal.at[:, mine], s_send, s_recv, partner)
+        return remote(dop.at[0, :, pl.ds(0, width)], scal.at[:, mine], s_send, s_recv, partner)
 
     def scaling_chip(k):
         to = {"tile": 2 * (1 - y) + lax.rem(c + k, 2)}
@@ -742,30 +746,61 @@
             p_send.at[k], p_recv.at[k], to,
         )
 
-    def far_rows(g):
-        return far.at[pl.ds(pl.multiple_of(g * part, part), part), :]
+    def turn_part(ref, base, z, s):
+        first = base + (z * n_strip + s) * part
+        return ref.at[:, pl.ds(pl.multiple_of(first, part), part), :]
 
     def scal_rows(g):
         return scal.at[pl.ds(pl.multiple_of(g * block, block), block), other]
 
     def range_chip():
-        return remote(for_range, far_rows(slab), p_send.at[2], p_recv.at[2], across)
+        return remote(
+            turn_part(swap, 0, az, strip), turn_part(turn, y * half, az, strip),
+            p_send.at[2], p_recv.at[2], across,
+        )
+
+    def slice_of(z, k):
+        if k:
+            return turn_part(turn, (1 - y) * half, z, strip)
+        return scal_rows(strip * n_az + z)
 
     def along(d, z, k):
         to = {"az": lax.rem(az + d, n_az)}
-        at = (scal_rows, far_rows)[k](strip * n_az + z)
+        at = slice_of(z, k)
         return remote(at, at, az_send.at[d, k], az_recv.at[z, k], to)
 
+    def up(i, k):
+        at = slice_of(az - i, k)
+        return remote(at, at, up_send.at[i, k], az_recv.at[az - i, k], {"az": lax.rem(az + 1, n_az)})
+
+    def relay(i):
+        @pl.when(az >= i)
+        def _():
+            for k in (0, 1):
+                along(1, az - i, k).wait_recv()
+                sideways(az - i, k).start()
+
+                @pl.when(az + 1 < n_az)
+                def _():
+                    up(i, k).start()
+
     def sideways(z, k):
-        at = (scal_rows, far_rows)[k](strip * n_az + z)
+        at = slice_of(z, k)
         return remote(at, at, x_send.at[z, k], x_recv.at[z, k], {"strip": 1 - strip})
+
+    def share(k):
+        sideways(az, k).start()
+        for d in range(n_az - 1, 0, -1):
+            @pl.when(az + d >= n_az)
+            def _():
+                along(d, az, k).start()
 
     def order(n):
         return jnp.where(az + n < n_az, az + n, n_az - 1 - n)
 
     def place(n):
-        s = jnp.where(n < n_az, y, 1 - y)
-        z = order(lax.rem(n, n_az))
+        s = jnp.where(lax.rem(n, 2) == 0, y, 1 - y)
+        z = order(n // 2)
         base = (s * n_az + z) * block
         row = (2 * s + c) * m + y * half + z * block
         return pl.ds(pl.multiple_of(base, block), block), pl.ds(pl.multiple_of(row, block), block), base
@@ -805,10 +840,6 @@
     @pl.loop(0, spans)
     def _(j):
         own_phase(scaling_ref, j, 0).start()
-
-    @pl.loop(0, n_one)
-    def _(a):
-        own_range(a).start()
 
     @pl.loop(0, n_one)
     def _(a):
@@ -843,27 +874,18 @@
 
     for k in (0, 1):
         scaling_chip(k).start()
-
-    @pl.loop(0, n_one)
-    def _(g):
-        own_range(g).wait()
-        for_range[:, lanes(g)] = turn[g, pl.ds(2 * part * slab + 1 - y, part, stride=2), :]
-
-    range_chip().start()
-
     @pl.loop(0, spans)
     def _(j):
         for h in (0, 1):
             rows = pl.ds(h * half, half)
-            for_core[rows, lanes(j)] = phase[j, pl.ds((2 * h + 1 - c) * m + y, half, stride=2), :]
+            dop[0, rows, lanes(j)] = phase[j, pl.ds((2 * h + 1 - c) * m + y, half, stride=2), :]
             scal[rows, lanes(t * spans + j)] = phase[j, pl.ds((2 * h + c) * m + y, half, stride=2), :]
 
     scaling_core().start()
-    turn_rows(lambda g: turn[g, pl.ds(y, half, stride=2), :], mid, turn, y * half)
-
-    @pl.loop(0, spans)
-    def _(j):
-        own_phase(azimuth_ref, j, 1).start()
+
+    @pl.loop(0, n_one)
+    def _(a):
+        own_range(a).start()
 
     for k in range(6):
         twist_ref[k] = jnp.broadcast_to(twists_ref[:, k : k + 1], (m, LANES))
@@ -872,6 +894,7 @@
         for i in range(1, tiles):
             x = jnp.where(t == i, twists_ref[pl.ds(0, half), 6 + 2 * i + k : 7 + 2 * i + k], x)
         turn_front[k] = jnp.broadcast_to(x, (half, LANES))
+    scaling_core().wait_send()
     get_front.wait()
     odd = lax.rem(lax.broadcasted_iota(jnp.int32, (1, pulses), 1), 2) * c
     for k in (0, 1):
@@ -898,15 +921,40 @@
             echo_across(j).start()
             echo_core(j).start()
 
-        @pl.when(j == 4)
+        @pl.when(j == 2)
         def _():
             for k in (0, 1):
                 scaling_chip(k).wait_recv()
+            share(0)
+
+        @pl.when(j == 3)
+        def _():
+            @pl.loop(0, n_one)
+            def _(a):
+                own_range(a).wait()
+
+            turn_rows(lambda g: range_piece(g, 1 - y, half, 2)[...], mid, swap, 0)
+            range_chip().start()
+
+        @pl.when(j == 5)
+        def _():
+            turn_rows(lambda g: range_piece(g, y, half, 2)[...], mid, turn, y * half)
+
+            @pl.loop(0, spans)
+            def _(i):
+                own_phase(azimuth_ref, i, 1).start()
+
+        @pl.when(j == 8)
+        def _():
             range_chip().wait_recv()
-            for k in (0, 1):
-                sideways(az, k).start()
-                for d in range(n_az - 1, 0, -1):
-                    along(d, az, k).start()
+            share(1)
+
+        @pl.when(j == chunks - 1)
+        def _():
+            @pl.when(az + 1 < n_az)
+            def _():
+                for k in (0, 1):
+                    up(0, k).start()
 
         for d in range(1, n_az):
             @pl.when((j == chunks - n_az + d - 1) & (az + d < n_az))
@@ -914,11 +962,6 @@
                 for k in (0, 1):
                     along(n_az - d, az + d, k).wait_recv()
                     sideways(az + d, k).start()
-
-        @pl.when((j >= 2) & (j < chunks + 2))
-        def _():
-            echo_across(j - 2).wait_recv()
-            echo_forward(j - 2).start()
 
         @pl.when(j >= 3)
         def _():
@@ -947,26 +990,28 @@
                 dop[k, pl.ds(0, half), at] = a + b
                 dop[k, pl.ds(half, half), at] = a - b
 
+        @pl.when((j >= 2) & (j < chunks + 2))
+        def _():
+            echo_across(j - 2).wait_recv()
+            echo_forward(j - 2).start()
+
+        @pl.when(j == chunks + 1)
+        def _():
+            relay(1)
+
     scaling_core().wait_recv()
 
     @pl.loop(0, blocks)
     def _(n):
-        @pl.when(n < n_az)
-        def _():
-            z = order(n)
-
-            @pl.when(az + n >= n_az)
+        for i in range(2, n_az):
+            @pl.when(n == 2 * i - 3)
             def _():
-                for k in (0, 1):
-                    along(n_az - 1, z, k).wait_recv()
-                    sideways(z, k).start()
-
+                relay(i)
+
+        @pl.when(lax.rem(n, 2) == 0)
+        def _():
             for k in (0, 1):
-                sideways(z, k).wait_recv()
-
-        @pl.when(n == n_az)
-        def _():
-            turn_rows(lambda g: far[:, lanes(g)], mid, turn, (1 - y) * half)
+                sideways(order(n // 2), k).wait_recv()
 
         filter_block(
             dop, place(n)[2], block, scal, fwd_ref, inv_ref, range_twist_ref, turn, hi_ref, lo_ref, mid
@@ -1038,12 +1083,17 @@
         echo_core(j).wait_send()
         echo_forward(j).wait_send()
 
-    scaling_core().wait_send()
     range_chip().wait_send()
     for k in (0, 1):
         scaling_chip(k).wait_send()
         for d in range(1, n_az):
-            along(d, az, k).wait_send()
+            @pl.when(az + d >= n_az)
+            def _():
+                along(d, az, k).wait_send()
+
+            @pl.when((az + 1 < n_az) & (az >= d - 1))
+            def _():
+                up(d - 1, k).wait_send()
         for z in range(n_az):
             sideways(z, k).wait_send()
     for n in range(whole):
@@ -1087,13 +1137,11 @@
             pltpu.VMEM((n_one, 2, pulses // tiles, LANES), F32),
             pltpu.VMEM((2, count, ranges), F32),
             pltpu.VMEM((count, ranges), F32),
-            pltpu.VMEM((half, ranges), F32),
+            pltpu.VMEM((n_one, half, LANES), F32),
             pltpu.VMEM((n_one, count, LANES), F32),
             pltpu.VMEM((spans, extent, LANES), F32),
             pltpu.VMEM((2, extent, width), F32),
-            pltpu.VMEM((count, width), F32),
             pltpu.VMEM((2, block, width), F32),
-            pltpu.VMEM((half // blocks, ranges), F32),
             pltpu.VMEM((2, count, pulses), BF16),
             pltpu.VMEM((2, half, LANES), F32),
             pltpu.VMEM((6, m, LANES), F32),
@@ -1108,14 +1156,14 @@
             dma((chunks,)), dma((chunks,)),
             dma, dma,
             dma((3,)), dma((3,)),
-            dma((n_az, 2)), dma((n_az, 2)),
+            dma((n_az, 2)), dma((n_az, 2)), dma((n_az, 2)),
             dma((n_az, 2)), dma((n_az, 2)),
             dma((whole, tiles - 1)), dma((whole, tiles - 1)), dma((whole,)),
             dma((spans, rest, tiles - 1)), dma((spans, rest, tiles - 1)), dma((spans, rest)),
             dma((2,)),
         ],
         compiler_params=pltpu.CompilerParams(
-            collective_id=0, has_side_effects=True, vmem_limit_bytes=63 << 20
+            collective_id=0, has_side_effects=True, vmem_limit_bytes=59 << 20
         ),
     )(
         raw_echo,

time: 240 us -> 221 us (0.921)
  Pallas kernels: 235 us -> 215 us
    pallas_call x1, Pallas kernels: 235 us -> 215 us  [pair_body(): pl.pallas_call(functools.partial(pair_kernel, n_strip, n_az, block, chunk...]
where the time goes in v3:
time: 221 us; the launch traced here: 220 us
  Pallas kernels  215 us (97%)
  local copies, waits for them, and re-layouts  4.79 us (2%)
    pallas_call x1, Pallas kernels, pair_body(): pl.pallas_call(functools.partial(pair_kernel, n_strip, n_az, block, chunk...  215 us
    unnamed x1, local copies, waits for them, and re-layouts  4.79 us

profile of v3, /device:TPU:16, one launch (start us, length us, event | category | flops | bytes accessed | tf_op | source)
XLA Modules:
  0.0 219.7 jit_solution(3729449734883242228)
XLA Ops:
  0.0 214.9 %shard_map.100 = f32[2,512,1024]{2,1,0:T(8,128)} custom-call(f32[2,128,4096]{2,1,0:T(8,128)} %raw_ref.1, f32[1024,1024]{1,0:T(8,128)} %scaling_ref.1, f32[256,4096]{1,0:T(8,128)} %range_ref.1, f32[1024,1024]{1,0:T(8,128)} %azimuth_ref.1, bf16[2,2,256,512]{3,2,1,0:T(8,128)(2,1)} %constant.12.clone.front_ref, f32[256,128]{1,0:T(8,128)} %constant.13.clone.twists_ref, ...), custom_call_target="tpu_custom_call" | custom-call | tf_op jit(solution)/shard_map/pallas_call | solution.py:1130
  214.9 4.8 %copy.12 = f32[2,512,1024]{2,1,0:T(8,128)} copy(f32[2,512,1024]{2,1,0:T(8,128)} %shard_map.100) | data formatting | bytes 8388608

commit v4 on v3

--- a/solution.py
+++ b/solution.py
@@ -682,7 +682,9 @@
     chunks = n_one // chunk
     blocks = count // block
     part = half // blocks
-    whole = blocks // 2 + 1
+    whole = blocks - 2
+    lag, steps = 2, 2
+    step = block // steps
     partner, across = {"tile": 2 * y + 1 - c}, {"tile": 2 * (1 - y) + c}
     other = pl.ds(pl.multiple_of(2 * (1 - y) * width, LANES), 2 * width)
     mine = pl.ds(pl.multiple_of(t * width, LANES), width)
@@ -803,30 +805,35 @@
         z = order(n // 2)
         base = (s * n_az + z) * block
         row = (2 * s + c) * m + y * half + z * block
-        return pl.ds(pl.multiple_of(base, block), block), pl.ds(pl.multiple_of(row, block), block), base
-
-    def back(n, k):
+        return pl.ds(pl.multiple_of(base, block), block), pl.ds(pl.multiple_of(row, block), block), base, row
+
+    def piece_rows(u):
+        _, _, base, row = place(u // steps)
+        first = lax.rem(u, steps) * step
+        return tuple(pl.ds(pl.multiple_of(x + first, step), step) for x in (base, row))
+
+    def back(u, k):
         to = lax.rem(t + k, tiles)
-        src, dst, _ = place(n)
+        src, dst = piece_rows(u)
         at = pl.ds(pl.multiple_of(to * width, LANES), width)
         return remote(
-            dop.at[:, src, at], ret.at[:, dst, :], w_send.at[n, k - 1], w_recv.at[n, k - 1], {"tile": to}
-        )
-
-    def keep(n):
-        src, dst, _ = place(n)
-        return pltpu.make_async_copy(dop.at[:, src, mine], ret.at[:, dst, :], w_local.at[n])
+            dop.at[:, src, at], ret.at[:, dst, :], w_send.at[u, k - 1], w_recv.at[u, k - 1], {"tile": to}
+        )
+
+    def keep(u):
+        src, dst = piece_rows(u)
+        return pltpu.make_async_copy(dop.at[:, src, mine], ret.at[:, dst, :], w_local.at[u])
 
     def back_span(j, n, k):
         to = lax.rem(t + k, tiles)
-        src, dst, _ = place(n)
+        src, dst, _, _ = place(n)
         return remote(
             dop.at[:, src, lanes(to * spans + j)], ret.at[:, dst, lanes(j)],
             v_send.at[j, n - whole, k - 1], v_recv.at[j, n - whole, k - 1], {"tile": to},
         )
 
     def keep_span(j, n):
-        src, dst, _ = place(n)
+        src, dst, _, _ = place(n)
         return pltpu.make_async_copy(
             dop.at[:, src, lanes(t * spans + j)], ret.at[:, dst, lanes(j)], v_local.at[j, n - whole]
         )
@@ -901,7 +908,7 @@
         front[k] = (front[k].astype(F32) * (1 - 2 * odd).astype(F32)).astype(BF16)
     sign = (1 - 2 * y).astype(F32)
 
-    @pl.loop(0, chunks + 3)
+    @pl.loop(0, chunks + lag + 1)
     def _(j):
         @pl.when(j < chunks)
         def _():
@@ -963,9 +970,9 @@
                     along(n_az - d, az + d, k).wait_recv()
                     sideways(az + d, k).start()
 
-        @pl.when(j >= 3)
-        def _():
-            now = j - 3
+        @pl.when(j > lag)
+        def _():
+            now = j - lag - 1
             echo_core(now).wait_recv()
             echo_forward(now).wait_recv()
             r = []
@@ -990,38 +997,39 @@
                 dop[k, pl.ds(0, half), at] = a + b
                 dop[k, pl.ds(half, half), at] = a - b
 
-        @pl.when((j >= 2) & (j < chunks + 2))
-        def _():
-            echo_across(j - 2).wait_recv()
-            echo_forward(j - 2).start()
-
-        @pl.when(j == chunks + 1)
+        @pl.when((j >= lag) & (j < chunks + lag))
+        def _():
+            echo_across(j - lag).wait_recv()
+            echo_forward(j - lag).start()
+
+        @pl.when(j == chunks + lag - 1)
         def _():
             relay(1)
 
     scaling_core().wait_recv()
 
-    @pl.loop(0, blocks)
-    def _(n):
+    @pl.loop(0, blocks * steps)
+    def _(u):
         for i in range(2, n_az):
-            @pl.when(n == 2 * i - 3)
+            @pl.when(u == steps * (2 * i - 3))
             def _():
                 relay(i)
 
-        @pl.when(lax.rem(n, 2) == 0)
+        @pl.when(lax.rem(u, 2 * steps) == 0)
         def _():
             for k in (0, 1):
-                sideways(order(n // 2), k).wait_recv()
+                sideways(order(u // (2 * steps)), k).wait_recv()
 
         filter_block(
-            dop, place(n)[2], block, scal, fwd_ref, inv_ref, range_twist_ref, turn, hi_ref, lo_ref, mid
-        )
-
-        @pl.when(n < whole)
+            dop, place(u // steps)[2] + lax.rem(u, steps) * step, step,
+            scal, fwd_ref, inv_ref, range_twist_ref, turn, hi_ref, lo_ref, mid,
+        )
+
+        @pl.when(u < whole * steps)
         def _():
             for k in range(tiles - 1, 0, -1):
-                back(n, k).start()
-            keep(n).start()
+                back(u, k).start()
+            keep(u).start()
 
     @pl.loop(0, spans)
     def _(j):
@@ -1034,10 +1042,11 @@
     def _(j):
         own_phase(azimuth_ref, j, 1).wait()
 
-    for n in range(whole):
+    @pl.loop(0, whole * steps)
+    def _(u):
         for k in range(1, tiles):
-            back(n, k).wait_recv()
-        keep(n).wait()
+            back(u, k).wait_recv()
+        keep(u).wait()
 
     @pl.loop(0, spans)
     def _(j):
@@ -1096,9 +1105,11 @@
                 up(d - 1, k).wait_send()
         for z in range(n_az):
             sideways(z, k).wait_send()
-    for n in range(whole):
+
+    @pl.loop(0, whole * steps)
+    def _(u):
         for k in range(1, tiles):
-            back(n, k).wait_send()
+            back(u, k).wait_send()
 
     @pl.loop(0, spans)
     def _(j):
@@ -1119,7 +1130,7 @@
     block = count // blocks
     chunk = 2
     chunks = n_one // chunk
-    whole = blocks // 2 + 1
+    whole = blocks - 2
     rest = blocks - whole
     fine = np.concatenate([np.arange(0, m, 2), np.arange(1, m, 2)])
     lane = np.arange(LANES)
@@ -1129,9 +1140,9 @@
     c, s = roots(np.arange(n_one), lane, ranges, -1)
     return pl.pallas_call(
         functools.partial(pair_kernel, n_strip, n_az, block, chunk),
-        out_shape=jax.ShapeDtypeStruct((2, pulses, width), F32),
+        out_shape=pltpu.VMEM((2, pulses, width), F32),
         in_specs=[anyspace] * 5 + [vmem] * 5,
-        out_specs=anyspace,
+        out_specs=vmem,
         scratch_shapes=[
             pltpu.VMEM((n_one, 2, pulses, LANES), F32),
             pltpu.VMEM((n_one, 2, pulses // tiles, LANES), F32),
@@ -1146,8 +1157,8 @@
             pltpu.VMEM((2, half, LANES), F32),
             pltpu.VMEM((6, m, LANES), F32),
             pltpu.VMEM((2, 2, pulses, LANES), F32),
-            pltpu.VMEM((n_one, block, 2 * LANES), BF16),
-            pltpu.VMEM((n_one, block, 2 * LANES), BF16),
+            pltpu.VMEM((n_one, block // 2, 2 * LANES), BF16),
+            pltpu.VMEM((n_one, block // 2, 2 * LANES), BF16),
             pltpu.VMEM((2, n_one * LANES // 2, LANES), F32),
             dma((2, spans)), dma((n_one,)), dma((n_one,)), dma,
             dma((n_one,)), dma((n_one,)),
@@ -1158,7 +1169,7 @@
             dma((3,)), dma((3,)),
             dma((n_az, 2)), dma((n_az, 2)), dma((n_az, 2)),
             dma((n_az, 2)), dma((n_az, 2)),
-            dma((whole, tiles - 1)), dma((whole, tiles - 1)), dma((whole,)),
+            dma((2 * whole, tiles - 1)), dma((2 * whole, tiles - 1)), dma((2 * whole,)),
             dma((spans, rest, tiles - 1)), dma((spans, rest, tiles - 1)), dma((spans, rest)),
             dma((2,)),
         ],
@@ -1189,7 +1200,7 @@
         and n_az > 1
         and count == 2 * LANES
         and phase_scaling.shape[0] == 2 * raw_echo.shape[1] * tiles
-        and count % (16 * blocks) == 0
+        and count % (32 * blocks) == 0
         and phase_range.shape[1] % (2 * LANES) == 0
     )
 

time: 221 us -> 215 us (0.973)
  Pallas kernels: 215 us -> 212 us
  local copies, waits for them, and re-layouts: 4.79 us -> 2.02 us
    unnamed x1, local copies, waits for them, and re-layouts: 4.79 us -> 2.02 us
    pallas_call x1, Pallas kernels: 215 us -> 212 us  [pair_body(): pl.pallas_call(functools.partial(pair_kernel, n_strip, n_az, block, chunk...]
where the time goes in v4:
time: 215 us; the launch traced here: 214 us
  Pallas kernels  212 us (99%)
    pallas_call x1, Pallas kernels, pair_body(): pl.pallas_call(functools.partial(pair_kernel, n_strip, n_az, block, chunk...  212 us

profile of v4, /device:TPU:16, one launch (start us, length us, event | category | flops | bytes accessed | tf_op | source)
XLA Modules:
  0.0 214.3 jit_solution(6569269080244857040)
XLA Ops:
  0.0 212.2 %shard_map.100 = f32[2,512,1024]{2,1,0:T(8,128)S(1)} custom-call(f32[2,128,4096]{2,1,0:T(8,128)} %raw_ref.1, f32[1024,1024]{1,0:T(8,128)} %scaling_ref.1, f32[256,4096]{1,0:T(8,128)} %range_ref.1, f32[1024,1024]{1,0:T(8,128)} %azimuth_ref.1, bf16[2,2,256,512]{3,2,1,0:T(8,128)(2,1)} %constant.12.clone.front_ref, f32[256,128]{1,0:T(8,128)} %constant.13.clone.twists_ref, ...), custom_call_target="tpu_custom_call" | custom-call | tf_op jit(solution)/shard_map/pallas_call | solution.py:1141
  212.3 2.0 copy.12

commit v5 on v4

--- a/solution.py
+++ b/solution.py
@@ -636,18 +636,20 @@
                 x_ref[c, at, pl.ds(a * LANES, LANES)] = x[c]
 
 
-def turn_rows(load, mid, turn, base):
-    n_one = turn.shape[0]
-    half = n_one * LANES // 2
-    part = half // n_one
-    per = half // LANES
-    at = pl.ds(pl.multiple_of(base, LANES), LANES)
-
-    @pl.loop(0, n_one)
+def turn_in(load, mid, start, stop):
+    per = mid.shape[1] // LANES
+
+    @pl.loop(start, stop)
     def _(g):
         mid[g // per, pl.ds(pl.multiple_of(g % per * LANES, LANES), LANES), :] = load(g).T
 
-    @pl.loop(0, n_one)
+
+def turn_out(mid, turn, base, start, stop):
+    n_one = turn.shape[0]
+    part = mid.shape[1] // n_one
+    at = pl.ds(pl.multiple_of(base, LANES), LANES)
+
+    @pl.loop(start, stop)
     def _(k):
         rows = pl.ds(k, part, stride=n_one)
         x = jnp.concatenate([mid[h, rows, :] for h in range(LANES // part)], axis=0)
@@ -682,6 +684,7 @@
     chunks = n_one // chunk
     blocks = count // block
     part = half // blocks
+    parts = chunks // 4
     whole = blocks - 2
     lag, steps = 2, 2
     step = block // steps
@@ -725,8 +728,7 @@
 
     def echo_across(j):
         return remote(
-            prev.at[groups(j)], cols.at[groups(j), :, pulse_rows(t), :],
-            y_send.at[j], y_recv.at[j], across,
+            prev.at[j], cols.at[j, :, pulse_rows(t), :], y_send.at[j], y_recv.at[j], across,
         )
 
     def echo_core(j):
@@ -775,16 +777,21 @@
         at = slice_of(az - i, k)
         return remote(at, at, up_send.at[i, k], az_recv.at[az - i, k], {"az": lax.rem(az + 1, n_az)})
 
-    def relay(i):
+    def relay(i, k):
         @pl.when(az >= i)
         def _():
-            for k in (0, 1):
-                along(1, az - i, k).wait_recv()
-                sideways(az - i, k).start()
-
-                @pl.when(az + 1 < n_az)
-                def _():
-                    up(i, k).start()
+            along(1, az - i, k).wait_recv()
+            sideways(az - i, k).start()
+
+            @pl.when(az + 1 < n_az)
+            def _():
+                up(i, k).start()
+
+    def hand_over(d, k):
+        @pl.when(az + d < n_az)
+        def _():
+            along(n_az - d, az + d, k).wait_recv()
+            sideways(az + d, k).start()
 
     def sideways(z, k):
         at = slice_of(z, k)
@@ -801,8 +808,8 @@
         return jnp.where(az + n < n_az, az + n, n_az - 1 - n)
 
     def place(n):
-        s = jnp.where(lax.rem(n, 2) == 0, y, 1 - y)
-        z = order(n // 2)
+        s = jnp.where(n < n_az, y, 1 - y)
+        z = order(lax.rem(n, n_az))
         base = (s * n_az + z) * block
         row = (2 * s + c) * m + y * half + z * block
         return pl.ds(pl.multiple_of(base, block), block), pl.ds(pl.multiple_of(row, block), block), base, row
@@ -925,7 +932,7 @@
                     b = prev[at, k] * sign
                     cols[at, k, pulse_rows(t), :] = a + b
                     prev[at, k] = a - b
-            echo_across(j).start()
+                echo_across(at).start()
             echo_core(j).start()
 
         @pl.when(j == 2)
@@ -934,41 +941,52 @@
                 scaling_chip(k).wait_recv()
             share(0)
 
-        @pl.when(j == 3)
+        @pl.when(j == 1)
         def _():
             @pl.loop(0, n_one)
             def _(a):
                 own_range(a).wait()
 
-            turn_rows(lambda g: range_piece(g, 1 - y, half, 2)[...], mid, swap, 0)
-            range_chip().start()
-
-        @pl.when(j == 5)
-        def _():
-            turn_rows(lambda g: range_piece(g, y, half, 2)[...], mid, turn, y * half)
-
+        few = n_one // parts
+
+        @pl.when((j >= 1) & (j < 1 + parts))
+        def _():
+            i = (j - 1) * few
+            turn_in(lambda g: range_piece(g, 1 - y, half, 2)[...], mid, i, i + few)
+
+        @pl.when((j >= 1 + parts) & (j < 1 + 2 * parts))
+        def _():
+            i = (j - 1 - parts) * few
+            turn_out(mid, swap, 0, i, i + few)
+
+        @pl.when((j >= 1 + 2 * parts) & (j < 1 + 3 * parts))
+        def _():
+            i = (j - 1 - 2 * parts) * few
+            turn_in(lambda g: range_piece(g, y, half, 2)[...], mid, i, i + few)
+
+        @pl.when((j >= 1 + 3 * parts) & (j < 1 + 4 * parts))
+        def _():
+            i = (j - 1 - 3 * parts) * few
+            turn_out(mid, turn, y * half, i, i + few)
+
+        @pl.when(j == 1 + 4 * parts)
+        def _():
             @pl.loop(0, spans)
             def _(i):
                 own_phase(azimuth_ref, i, 1).start()
 
-        @pl.when(j == 8)
-        def _():
-            range_chip().wait_recv()
-            share(1)
-
         @pl.when(j == chunks - 1)
         def _():
+            range_chip().start()
+
             @pl.when(az + 1 < n_az)
             def _():
-                for k in (0, 1):
-                    up(0, k).start()
+                up(0, 0).start()
 
         for d in range(1, n_az):
-            @pl.when((j == chunks - n_az + d - 1) & (az + d < n_az))
+            @pl.when(j == chunks - n_az + d - 1)
             def _():
-                for k in (0, 1):
-                    along(n_az - d, az + d, k).wait_recv()
-                    sideways(az + d, k).start()
+                hand_over(d, 0)
 
         @pl.when(j > lag)
         def _():
@@ -999,26 +1017,43 @@
 
         @pl.when((j >= lag) & (j < chunks + lag))
         def _():
-            echo_across(j - lag).wait_recv()
+            for i in range(chunk):
+                echo_across((j - lag) * chunk + i).wait_recv()
             echo_forward(j - lag).start()
 
         @pl.when(j == chunks + lag - 1)
         def _():
-            relay(1)
+            relay(1, 0)
 
     scaling_core().wait_recv()
 
     @pl.loop(0, blocks * steps)
     def _(u):
         for i in range(2, n_az):
-            @pl.when(u == steps * (2 * i - 3))
+            @pl.when(u == steps * (i - 1) - 1)
             def _():
-                relay(i)
-
-        @pl.when(lax.rem(u, 2 * steps) == 0)
-        def _():
-            for k in (0, 1):
-                sideways(order(u // (2 * steps)), k).wait_recv()
+                relay(i, 0)
+
+        @pl.when((lax.rem(u, steps) == 0) & (u < n_az * steps))
+        def _():
+            sideways(order(u // steps), 0).wait_recv()
+
+        @pl.when(u == 1)
+        def _():
+            range_chip().wait_recv()
+            share(1)
+
+            @pl.when(az + 1 < n_az)
+            def _():
+                up(0, 1).start()
+
+        @pl.when(u == n_az * steps)
+        def _():
+            for i in range(1, n_az):
+                hand_over(i, 1)
+                relay(i, 1)
+            for i in range(n_az):
+                sideways(order(i), 1).wait_recv()
 
         filter_block(
             dop, place(u // steps)[2] + lax.rem(u, steps) * step, step,
@@ -1088,7 +1123,8 @@
 
     @pl.loop(0, chunks)
     def _(j):
-        echo_across(j).wait_send()
+        for i in range(chunk):
+            echo_across(j * chunk + i).wait_send()
         echo_core(j).wait_send()
         echo_forward(j).wait_send()
 
@@ -1162,7 +1198,7 @@
             pltpu.VMEM((2, n_one * LANES // 2, LANES), F32),
             dma((2, spans)), dma((n_one,)), dma((n_one,)), dma,
             dma((n_one,)), dma((n_one,)),
-            dma((chunks,)), dma((chunks,)),
+            dma((n_one,)), dma((n_one,)),
             dma((chunks,)), dma((chunks,)),
             dma((chunks,)), dma((chunks,)),
             dma, dma,
@@ -1201,7 +1237,7 @@
         and count == 2 * LANES
         and phase_scaling.shape[0] == 2 * raw_echo.shape[1] * tiles
         and count % (32 * blocks) == 0
-        and phase_range.shape[1] % (2 * LANES) == 0
+        and phase_range.shape[1] % (8 * LANES) == 0
     )
 
 

time: 215 us -> 210 us (0.977)
  Pallas kernels: 212 us -> 206 us
    pallas_call x1, Pallas kernels: 212 us -> 206 us  [pair_body(): pl.pallas_call(functools.partial(pair_kernel, n_strip, n_az, block, chunk...]
where the time goes in v5:
time: 210 us; the launch traced here: 208 us
  Pallas kernels  206 us (98%)
    pallas_call x1, Pallas kernels, pair_body(): pl.pallas_call(functools.partial(pair_kernel, n_strip, n_az, block, chunk...  206 us

profile of v5, /device:TPU:16, one launch (start us, length us, event | category | flops | bytes accessed | tf_op | source)
XLA Modules:
  0.0 208.2 jit_solution(6043136955761685389)
XLA Ops:
  0.0 206.2 %shard_map.100 = f32[2,512,1024]{2,1,0:T(8,128)S(1)} custom-call(f32[2,128,4096]{2,1,0:T(8,128)} %raw_ref.1, f32[1024,1024]{1,0:T(8,128)} %scaling_ref.1, f32[256,4096]{1,0:T(8,128)} %range_ref.1, f32[1024,1024]{1,0:T(8,128)} %azimuth_ref.1, bf16[2,2,256,512]{3,2,1,0:T(8,128)(2,1)} %constant.12.clone.front_ref, f32[256,128]{1,0:T(8,128)} %constant.13.clone.twists_ref, ...), custom_call_target="tpu_custom_call" | custom-call | tf_op jit(solution)/shard_map/pallas_call | solution.py:1177
  206.2 2.0 copy.12

commit v6 on v5

--- a/solution.py
+++ b/solution.py
@@ -659,12 +659,13 @@
 def pair_kernel(
     n_strip, n_az, block, chunk,
     raw_ref, scaling_ref, range_ref, azimuth_ref, front_ref,
+    twists_any, fwd_any, inv_any, range_twist_any, table_any,
+    o_ref,
     twists_ref, fwd_ref, inv_ref, range_twist_ref, table_ref,
-    o_ref,
     cols, prev, dop, scal, swap, turn, phase, ret, for_chip,
-    front, turn_front, twist_ref, head, hi_ref, lo_ref, mid,
-    load, load_range, load_echo, load_front, z_send, z_recv, y_send, y_recv, c_send, c_recv, f_send, f_recv,
-    s_send, s_recv, p_send, p_recv, az_send, up_send, az_recv, x_send, x_recv,
+    front, turn_front, twist_ref, spin, head, hi_ref, lo_ref, mid,
+    load, load_range, load_echo, load_front, load_table, z_send, z_recv, y_send, y_recv, c_send, c_recv, f_send, f_recv,
+    s_send, s_recv, p_send, p_recv, down_send, up_send, az_recv, x_send, x_recv,
     w_send, w_recv, w_local, v_send, v_recv, v_local, out_sem,
 ):
     t = lax.axis_index("tile")
@@ -768,19 +769,24 @@
             return turn_part(turn, (1 - y) * half, z, strip)
         return scal_rows(strip * n_az + z)
 
-    def along(d, z, k):
-        to = {"az": lax.rem(az + d, n_az)}
-        at = slice_of(z, k)
-        return remote(at, at, az_send.at[d, k], az_recv.at[z, k], to)
-
     def up(i, k):
         at = slice_of(az - i, k)
         return remote(at, at, up_send.at[i, k], az_recv.at[az - i, k], {"az": lax.rem(az + 1, n_az)})
 
+    def arrived(z, k):
+        at = slice_of(z, k)
+        remote(at, at, up_send.at[0, k], az_recv.at[z, k], {"az": lax.rem(az + 1, n_az)}).wait_recv()
+
+    def down(i, k):
+        at = slice_of(az + i, k)
+        return remote(
+            at, at, down_send.at[i, k], az_recv.at[az + i, k], {"az": lax.rem(az + n_az - 1, n_az)}
+        )
+
     def relay(i, k):
         @pl.when(az >= i)
         def _():
-            along(1, az - i, k).wait_recv()
+            arrived(az - i, k)
             sideways(az - i, k).start()
 
             @pl.when(az + 1 < n_az)
@@ -790,8 +796,12 @@
     def hand_over(d, k):
         @pl.when(az + d < n_az)
         def _():
-            along(n_az - d, az + d, k).wait_recv()
+            arrived(az + d, k)
             sideways(az + d, k).start()
+
+            @pl.when(az > 0)
+            def _():
+                down(d, k).start()
 
     def sideways(z, k):
         at = slice_of(z, k)
@@ -799,10 +809,10 @@
 
     def share(k):
         sideways(az, k).start()
-        for d in range(n_az - 1, 0, -1):
-            @pl.when(az + d >= n_az)
-            def _():
-                along(d, az, k).start()
+
+        @pl.when(az > 0)
+        def _():
+            down(0, k).start()
 
     def order(n):
         return jnp.where(az + n < n_az, az + n, n_az - 1 - n)
@@ -850,22 +860,51 @@
         return pltpu.make_async_copy(head.at[slot], o_ref.at[:, :, lanes(j)], out_sem.at[slot])
 
     get_front = pltpu.make_async_copy(front_ref.at[y], front, load_front)
-
-    @pl.loop(0, spans)
-    def _(j):
-        own_phase(scaling_ref, j, 0).start()
-
-    @pl.loop(0, n_one)
-    def _(a):
-        own_echo(a).start()
-
-    get_front.start()
+    get_tables = [
+        pltpu.make_async_copy(source, target, load_table.at[i])
+        for i, (source, target) in enumerate(
+            (
+                (twists_any, twists_ref),
+                (fwd_any, fwd_ref),
+                (inv_any, inv_ref),
+                (range_twist_any, range_twist_ref),
+                (table_any, table_ref),
+            )
+        )
+    ]
     barrier = greet(
         [{"tile": lax.rem(t + k, tiles)} for k in range(1, tiles)]
-        + [{"az": lax.rem(az + k, n_az)} for k in range(1, n_az)]
         + [{"strip": 1 - strip}]
     )
-    pl.semaphore_wait(barrier, tiles + n_az - 1)
+    neighbours = ((az + 1, az + 1 < n_az), (az + n_az - 1, az > 0))
+    for to, there in neighbours:
+        @pl.when(there)
+        def _():
+            pl.semaphore_signal(
+                barrier, inc=1, device_id={"az": lax.rem(to, n_az)}, device_id_type=pl.DeviceIdType.MESH
+            )
+
+
+    @pl.loop(0, spans)
+    def _(j):
+        own_phase(scaling_ref, j, 0).start()
+
+    @pl.when(az == 0)
+    def _():
+        @pl.loop(0, n_one)
+        def _(a):
+            prev[a] = jnp.zeros((2, rows_own, LANES), F32)
+
+    @pl.loop(0, spans)
+    def _(j):
+        own_phase(scaling_ref, j, 0).wait()
+        for k in (0, 1):
+            first = (2 * strip + k) * m + 2 * az * block + 1 - y
+            for_chip[k, :, lanes(j)] = phase[j, pl.ds(first, block, stride=2), :]
+
+    pl.semaphore_wait(barrier, tiles + sum(there.astype(jnp.int32) for _, there in neighbours))
+    for k in (0, 1):
+        scaling_chip(k).start()
 
     @pl.when(az < n_az - 1)
     def _():
@@ -873,21 +912,14 @@
         def _(a):
             onward(a).start()
 
-    @pl.when(az == 0)
-    def _():
-        @pl.loop(0, n_one)
-        def _(a):
-            prev[a] = jnp.zeros((2, rows_own, LANES), F32)
-
-    @pl.loop(0, spans)
-    def _(j):
-        own_phase(scaling_ref, j, 0).wait()
-        for k in (0, 1):
-            first = (2 * strip + k) * m + 2 * az * block + 1 - y
-            for_chip[k, :, lanes(j)] = phase[j, pl.ds(first, block, stride=2), :]
-
-    for k in (0, 1):
-        scaling_chip(k).start()
+    @pl.loop(0, n_one)
+    def _(a):
+        own_echo(a).start()
+
+    get_front.start()
+    for copy in get_tables:
+        copy.start()
+
     @pl.loop(0, spans)
     def _(j):
         for h in (0, 1):
@@ -901,6 +933,7 @@
     def _(a):
         own_range(a).start()
 
+    get_tables[0].wait()
     for k in range(6):
         twist_ref[k] = jnp.broadcast_to(twists_ref[:, k : k + 1], (m, LANES))
     for k in (0, 1):
@@ -984,7 +1017,7 @@
                 up(0, 0).start()
 
         for d in range(1, n_az):
-            @pl.when(j == chunks - n_az + d - 1)
+            @pl.when(j == 2 + chunks * d // n_az)
             def _():
                 hand_over(d, 0)
 
@@ -1021,11 +1054,10 @@
                 echo_across((j - lag) * chunk + i).wait_recv()
             echo_forward(j - lag).start()
 
-        @pl.when(j == chunks + lag - 1)
-        def _():
-            relay(1, 0)
-
+    relay(1, 0)
     scaling_core().wait_recv()
+    for copy in get_tables[1:]:
+        copy.wait()
 
     @pl.loop(0, blocks * steps)
     def _(u):
@@ -1047,11 +1079,14 @@
             def _():
                 up(0, 1).start()
 
-        @pl.when(u == n_az * steps)
-        def _():
-            for i in range(1, n_az):
+        for i in range(1, n_az):
+            @pl.when(u == steps * (i + 1))
+            def _():
                 hand_over(i, 1)
                 relay(i, 1)
+
+        @pl.when(u == n_az * steps)
+        def _():
             for i in range(n_az):
                 sideways(order(i), 1).wait_recv()
 
@@ -1085,6 +1120,11 @@
 
     @pl.loop(0, spans)
     def _(j):
+        for f in range(4):
+            angle = jnp.concatenate(
+                [phase[j, pl.ds(f * m + p, half, stride=2), :] for p in (0, 1)], axis=0
+            )
+            spin[0, f], spin[1, f] = sincos(angle)
         for n in range(whole, blocks):
             for k in range(1, tiles):
                 back_span(j, n, k).wait_recv()
@@ -1099,10 +1139,7 @@
         v = []
         for f in range(4):
             rows = pl.ds(f * m, m)
-            angle = jnp.concatenate(
-                [phase[j, pl.ds(f * m + p, half, stride=2), :] for p in (0, 1)], axis=0
-            )
-            v.append(times((ret[0, rows, lanes(j)], ret[1, rows, lanes(j)]), sincos(angle)))
+            v.append(times((ret[0, rows, lanes(j)], ret[1, rows, lanes(j)]), (spin[0, f], spin[1, f])))
         for e, x in enumerate(four(v, 1)):
             if e:
                 x = times(x, (twist_ref[2 * e - 2], twist_ref[2 * e - 1]))
@@ -1132,9 +1169,9 @@
     for k in (0, 1):
         scaling_chip(k).wait_send()
         for d in range(1, n_az):
-            @pl.when(az + d >= n_az)
+            @pl.when((az > 0) & (az + d - 1 < n_az))
             def _():
-                along(d, az, k).wait_send()
+                down(d - 1, k).wait_send()
 
             @pl.when((az + 1 < n_az) & (az >= d - 1))
             def _():
@@ -1177,9 +1214,14 @@
     return pl.pallas_call(
         functools.partial(pair_kernel, n_strip, n_az, block, chunk),
         out_shape=pltpu.VMEM((2, pulses, width), F32),
-        in_specs=[anyspace] * 5 + [vmem] * 5,
+        in_specs=[anyspace] * 10,
         out_specs=vmem,
         scratch_shapes=[
+            pltpu.VMEM((m, LANES), F32),
+            pltpu.VMEM((2, 2 * LANES, 2 * LANES), BF16),
+            pltpu.VMEM((2, 2 * LANES, 2 * LANES), BF16),
+            pltpu.VMEM((2, n_one, LANES), F32),
+            pltpu.VMEM((2, 2 * q, 2 * m), BF16),
             pltpu.VMEM((n_one, 2, pulses, LANES), F32),
             pltpu.VMEM((n_one, 2, pulses // tiles, LANES), F32),
             pltpu.VMEM((2, count, ranges), F32),
@@ -1192,11 +1234,12 @@
             pltpu.VMEM((2, count, pulses), BF16),
             pltpu.VMEM((2, half, LANES), F32),
             pltpu.VMEM((6, m, LANES), F32),
+            pltpu.VMEM((2, 4, m, LANES), F32),
             pltpu.VMEM((2, 2, pulses, LANES), F32),
             pltpu.VMEM((n_one, block // 2, 2 * LANES), BF16),
             pltpu.VMEM((n_one, block // 2, 2 * LANES), BF16),
             pltpu.VMEM((2, n_one * LANES // 2, LANES), F32),
-            dma((2, spans)), dma((n_one,)), dma((n_one,)), dma,
+            dma((2, spans)), dma((n_one,)), dma((n_one,)), dma, dma((5,)),
             dma((n_one,)), dma((n_one,)),
             dma((n_one,)), dma((n_one,)),
             dma((chunks,)), dma((chunks,)),

time: 210 us -> 207 us (0.986)
  no operation moved by 1% of the time
where the time goes in v6:
time: 207 us
  Pallas kernels  205 us (99%)
    pallas_call x1, Pallas kernels, pair_body(): pl.pallas_call(functools.partial(pair_kernel, n_strip, n_az, block, chunk...  205 us

profile of v6, /device:TPU:16, one launch (start us, length us, event | category | flops | bytes accessed | tf_op | source)
XLA Modules:
  0.0 207.1 jit_solution(15075506187582271374)
XLA Ops:
  0.0 205.1 %shard_map.100 = f32[2,512,1024]{2,1,0:T(8,128)S(1)} custom-call(f32[2,128,4096]{2,1,0:T(8,128)} %raw_ref.1, f32[1024,1024]{1,0:T(8,128)} %scaling_ref.1, f32[256,4096]{1,0:T(8,128)} %range_ref.1, f32[1024,1024]{1,0:T(8,128)} %azimuth_ref.1, bf16[2,2,256,512]{3,2,1,0:T(8,128)(2,1)} %constant.12.clone.front_ref, f32[256,128]{1,0:T(8,128)} %constant.13.clone.twists_any, ...), custom_call_target="tpu_custom_call" | custom-call | tf_op jit(solution)/shard_map/pallas_call | solution.py:1214
  205.1 2.0 copy.12

commit v7 on v6

--- a/solution.py
+++ b/solution.py
@@ -586,11 +586,14 @@
     b_hi, b_lo = inv_ref[0], inv_ref[1]
     whole = pl.ds(pl.multiple_of(base, block), block)
 
-    @pl.loop(0, n_one)
+    wide = 8 * LANES
+
+    @pl.loop(0, n_one * LANES // wide)
     def _(a):
-        x = times((x_ref[0, whole, lanes(a)], x_ref[1, whole, lanes(a)]), sincos(scal_ref[whole, lanes(a)]))
-        x_ref[0, whole, lanes(a)] = x[0]
-        x_ref[1, whole, lanes(a)] = x[1]
+        at = pl.ds(pl.multiple_of(a * wide, wide), wide)
+        x = times((x_ref[0, whole, at], x_ref[1, whole, at]), sincos(scal_ref[whole, at]))
+        x_ref[0, whole, at] = x[0]
+        x_ref[1, whole, at] = x[1]
 
     @pl.loop(0, block // step)
     def _(i):
@@ -665,8 +668,8 @@
     cols, prev, dop, scal, swap, turn, phase, ret, for_chip,
     front, turn_front, twist_ref, spin, head, hi_ref, lo_ref, mid,
     load, load_range, load_echo, load_front, load_table, z_send, z_recv, y_send, y_recv, c_send, c_recv, f_send, f_recv,
-    s_send, s_recv, p_send, p_recv, down_send, up_send, az_recv, x_send, x_recv,
-    w_send, w_recv, w_local, v_send, v_recv, v_local, out_sem,
+    s_send, s_recv, p_send, p_recv, down_send, up_send, az_recv, swap_send, swap_recv, x_send, x_recv,
+    w_send, w_recv, w_local, v_send, v_recv, v_local,
 ):
     t = lax.axis_index("tile")
     az = lax.axis_index("az")
@@ -765,9 +768,13 @@
         )
 
     def slice_of(z, k):
-        if k:
+        if k == 1:
             return turn_part(turn, (1 - y) * half, z, strip)
-        return scal_rows(strip * n_az + z)
+        return scal_rows((y if k == 0 else 1 - y) * n_az + z)
+
+    def swap_scaling():
+        at = scal_rows(slab)
+        return remote(at, at, swap_send, swap_recv, {"strip": 1 - strip})
 
     def up(i, k):
         at = slice_of(az - i, k)
@@ -787,7 +794,8 @@
         @pl.when(az >= i)
         def _():
             arrived(az - i, k)
-            sideways(az - i, k).start()
+            if k == 1:
+                sideways(az - i).start()
 
             @pl.when(az + 1 < n_az)
             def _():
@@ -797,22 +805,16 @@
         @pl.when(az + d < n_az)
         def _():
             arrived(az + d, k)
-            sideways(az + d, k).start()
+            if k == 1:
+                sideways(az + d).start()
 
             @pl.when(az > 0)
             def _():
                 down(d, k).start()
 
-    def sideways(z, k):
-        at = slice_of(z, k)
-        return remote(at, at, x_send.at[z, k], x_recv.at[z, k], {"strip": 1 - strip})
-
-    def share(k):
-        sideways(az, k).start()
-
-        @pl.when(az > 0)
-        def _():
-            down(0, k).start()
+    def sideways(z):
+        at = slice_of(z, 1)
+        return remote(at, at, x_send.at[z], x_recv.at[z], {"strip": 1 - strip})
 
     def order(n):
         return jnp.where(az + n < n_az, az + n, n_az - 1 - n)
@@ -854,10 +856,6 @@
         return pltpu.make_async_copy(
             dop.at[:, src, lanes(t * spans + j)], ret.at[:, dst, lanes(j)], v_local.at[j, n - whole]
         )
-
-    def put(j):
-        slot = lax.rem(j, 2)
-        return pltpu.make_async_copy(head.at[slot], o_ref.at[:, :, lanes(j)], out_sem.at[slot])
 
     get_front = pltpu.make_async_copy(front_ref.at[y], front, load_front)
     get_tables = [
@@ -920,32 +918,6 @@
     for copy in get_tables:
         copy.start()
 
-    @pl.loop(0, spans)
-    def _(j):
-        for h in (0, 1):
-            rows = pl.ds(h * half, half)
-            dop[0, rows, lanes(j)] = phase[j, pl.ds((2 * h + 1 - c) * m + y, half, stride=2), :]
-            scal[rows, lanes(t * spans + j)] = phase[j, pl.ds((2 * h + c) * m + y, half, stride=2), :]
-
-    scaling_core().start()
-
-    @pl.loop(0, n_one)
-    def _(a):
-        own_range(a).start()
-
-    get_tables[0].wait()
-    for k in range(6):
-        twist_ref[k] = jnp.broadcast_to(twists_ref[:, k : k + 1], (m, LANES))
-    for k in (0, 1):
-        x = twists_ref[pl.ds(0, half), 6 + k : 7 + k]
-        for i in range(1, tiles):
-            x = jnp.where(t == i, twists_ref[pl.ds(0, half), 6 + 2 * i + k : 7 + 2 * i + k], x)
-        turn_front[k] = jnp.broadcast_to(x, (half, LANES))
-    scaling_core().wait_send()
-    get_front.wait()
-    odd = lax.rem(lax.broadcasted_iota(jnp.int32, (1, pulses), 1), 2) * c
-    for k in (0, 1):
-        front[k] = (front[k].astype(F32) * (1 - 2 * odd).astype(F32)).astype(BF16)
     sign = (1 - 2 * y).astype(F32)
 
     @pl.loop(0, chunks + lag + 1)
@@ -968,11 +940,52 @@
                 echo_across(at).start()
             echo_core(j).start()
 
+        @pl.when(j == 0)
+        def _():
+            @pl.loop(0, spans)
+            def _(i):
+                for h in (0, 1):
+                    rows = pl.ds(h * half, half)
+                    dop[0, rows, lanes(i)] = phase[i, pl.ds((2 * h + 1 - c) * m + y, half, stride=2), :]
+                    scal[rows, lanes(t * spans + i)] = phase[i, pl.ds((2 * h + c) * m + y, half, stride=2), :]
+
+            scaling_core().start()
+
+            @pl.loop(0, n_one)
+            def _(a):
+                own_range(a).start()
+
+            get_tables[0].wait()
+            for k in range(6):
+                twist_ref[k] = jnp.broadcast_to(twists_ref[:, k : k + 1], (m, LANES))
+            for k in (0, 1):
+                x = twists_ref[pl.ds(0, half), 6 + k : 7 + k]
+                for i in range(1, tiles):
+                    x = jnp.where(t == i, twists_ref[pl.ds(0, half), 6 + 2 * i + k : 7 + 2 * i + k], x)
+                turn_front[k] = jnp.broadcast_to(x, (half, LANES))
+
+        @pl.when(j == 1)
+        def _():
+            scaling_core().wait_send()
+            get_front.wait()
+            odd = lax.rem(lax.broadcasted_iota(jnp.int32, (1, pulses), 1), 2) * c
+            for k in (0, 1):
+                front[k] = (front[k].astype(F32) * (1 - 2 * odd).astype(F32)).astype(BF16)
+
         @pl.when(j == 2)
         def _():
             for k in (0, 1):
                 scaling_chip(k).wait_recv()
-            share(0)
+            swap_scaling().start()
+
+        @pl.when(j == 4)
+        def _():
+            swap_scaling().wait_recv()
+
+            @pl.when(az > 0)
+            def _():
+                for k in (0, 2):
+                    down(0, k).start()
 
         @pl.when(j == 1)
         def _():
@@ -1017,9 +1030,10 @@
                 up(0, 0).start()
 
         for d in range(1, n_az):
-            @pl.when(j == 2 + chunks * d // n_az)
-            def _():
-                hand_over(d, 0)
+            for k in (0, 2):
+                @pl.when(j == 2 + chunks * d // n_az + k // 2)
+                def _():
+                    hand_over(d, k)
 
         @pl.when(j > lag)
         def _():
@@ -1061,23 +1075,24 @@
 
     @pl.loop(0, blocks * steps)
     def _(u):
-        for i in range(2, n_az):
-            @pl.when(u == steps * (i - 1) - 1)
+        @pl.when(u == 1)
+        def _():
+            range_chip().wait_recv()
+            sideways(az).start()
+
+            @pl.when(az > 0)
             def _():
-                relay(i, 0)
-
-        @pl.when((lax.rem(u, steps) == 0) & (u < n_az * steps))
-        def _():
-            sideways(order(u // steps), 0).wait_recv()
-
-        @pl.when(u == 1)
-        def _():
-            range_chip().wait_recv()
-            share(1)
+                down(0, 1).start()
 
             @pl.when(az + 1 < n_az)
             def _():
                 up(0, 1).start()
+                up(0, 2).start()
+
+        for i in range(2, n_az):
+            @pl.when(u == steps * i)
+            def _():
+                relay(i, 0)
 
         for i in range(1, n_az):
             @pl.when(u == steps * (i + 1))
@@ -1085,10 +1100,14 @@
                 hand_over(i, 1)
                 relay(i, 1)
 
+            @pl.when(u == steps * (n_az + i - 1))
+            def _():
+                relay(i, 2)
+
         @pl.when(u == n_az * steps)
         def _():
             for i in range(n_az):
-                sideways(order(i), 1).wait_recv()
+                sideways(order(i)).wait_recv()
 
         filter_block(
             dop, place(u // steps)[2] + lax.rem(u, steps) * step, step,
@@ -1130,12 +1149,6 @@
                 back_span(j, n, k).wait_recv()
             keep_span(j, n).wait()
         hi, lo = table_ref[0], table_ref[1]
-        slot = lax.rem(j, 2)
-
-        @pl.when(j > 1)
-        def _():
-            put(j - 2).wait()
-
         v = []
         for f in range(4):
             rows = pl.ds(f * m, m)
@@ -1146,11 +1159,8 @@
             s_hi, s_lo = split(jnp.concatenate(x, axis=0))
             r = mm(hi, s_hi) + mm(hi, s_lo) + mm(lo, s_hi)
             for k in (0, 1):
-                head[slot, k, pl.ds(e, q, stride=4), :] = r[k * q : (k + 1) * q]
-        put(j).start()
-
-    for j in range(max(0, spans - 2), spans):
-        put(j).wait()
+                head[k, pl.ds(e, q, stride=4), :] = r[k * q : (k + 1) * q]
+        o_ref[:, :, lanes(j)] = head[...]
 
     @pl.when(az < n_az - 1)
     def _():
@@ -1168,16 +1178,18 @@
     range_chip().wait_send()
     for k in (0, 1):
         scaling_chip(k).wait_send()
-        for d in range(1, n_az):
-            @pl.when((az > 0) & (az + d - 1 < n_az))
+    swap_scaling().wait_send()
+    for z in range(n_az):
+        sideways(z).wait_send()
+    for k in (0, 1, 2):
+        for d in range(n_az - 1):
+            @pl.when((az > 0) & (az + d < n_az))
             def _():
-                down(d - 1, k).wait_send()
-
-            @pl.when((az + 1 < n_az) & (az >= d - 1))
+                down(d, k).wait_send()
+
+            @pl.when((az + 1 < n_az) & (az >= d))
             def _():
-                up(d - 1, k).wait_send()
-        for z in range(n_az):
-            sideways(z, k).wait_send()
+                up(d, k).wait_send()
 
     @pl.loop(0, whole * steps)
     def _(u):
@@ -1235,7 +1247,7 @@
             pltpu.VMEM((2, half, LANES), F32),
             pltpu.VMEM((6, m, LANES), F32),
             pltpu.VMEM((2, 4, m, LANES), F32),
-            pltpu.VMEM((2, 2, pulses, LANES), F32),
+            pltpu.VMEM((2, pulses, LANES), F32),
             pltpu.VMEM((n_one, block // 2, 2 * LANES), BF16),
             pltpu.VMEM((n_one, block // 2, 2 * LANES), BF16),
             pltpu.VMEM((2, n_one * LANES // 2, LANES), F32),
@@ -1246,11 +1258,11 @@
             dma((chunks,)), dma((chunks,)),
             dma, dma,
             dma((3,)), dma((3,)),
-            dma((n_az, 2)), dma((n_az, 2)), dma((n_az, 2)),
-            dma((n_az, 2)), dma((n_az, 2)),
+            dma((n_az, 3)), dma((n_az, 3)), dma((n_az, 3)),
+            dma, dma,
+            dma((n_az,)), dma((n_az,)),
             dma((2 * whole, tiles - 1)), dma((2 * whole, tiles - 1)), dma((2 * whole,)),
             dma((spans, rest, tiles - 1)), dma((spans, rest, tiles - 1)), dma((spans, rest)),
-            dma((2,)),
         ],
         compiler_params=pltpu.CompilerParams(
             collective_id=0, has_side_effects=True, vmem_limit_bytes=59 << 20

time: 207 us -> 206 us (level)
    pallas_call x1, Pallas kernels: 205 us -> 203 us  [pair_body(): pl.pallas_call(functools.partial(pair_kernel, n_strip, n_az, block, chunk...]
where the time goes in v7:
time: 206 us; the launch traced here: 205 us
  Pallas kernels  203 us (99%)
    pallas_call x1, Pallas kernels, pair_body(): pl.pallas_call(functools.partial(pair_kernel, n_strip, n_az, block, chunk...  203 us

profile of v7, /device:TPU:16, one launch (start us, length us, event | category | flops | bytes accessed | tf_op | source)
XLA Modules:
  0.0 204.7 jit_solution(17589902460237963585)
XLA Ops:
  0.0 202.7 %shard_map.100 = f32[2,512,1024]{2,1,0:T(8,128)S(1)} custom-call(f32[2,128,4096]{2,1,0:T(8,128)} %raw_ref.1, f32[1024,1024]{1,0:T(8,128)} %scaling_ref.1, f32[256,4096]{1,0:T(8,128)} %range_ref.1, f32[1024,1024]{1,0:T(8,128)} %azimuth_ref.1, bf16[2,2,256,512]{3,2,1,0:T(8,128)(2,1)} %constant.12.clone.front_ref, f32[256,128]{1,0:T(8,128)} %constant.13.clone.twists_any, ...), custom_call_target="tpu_custom_call" | custom-call | tf_op jit(solution)/shard_map/pallas_call | solution.py:1226
  202.7 2.0 copy.12

commit v8 on v7

--- a/solution.py
+++ b/solution.py
@@ -740,7 +740,7 @@
         return remote(at, at, c_send.at[j], c_recv.at[j], partner)
 
     def echo_forward(j):
-        at = cols.at[groups(j), :, pulse_rows(2 * (1 - y) + c), :]
+        at = cols.at[j, :, pulse_rows(2 * (1 - y) + c), :]
         return remote(at, at, f_send.at[j], f_recv.at[j], partner)
 
     def scaling_core():
@@ -1039,7 +1039,8 @@
         def _():
             now = j - lag - 1
             echo_core(now).wait_recv()
-            echo_forward(now).wait_recv()
+            for i in range(chunk):
+                echo_forward(now * chunk + i).wait_recv()
             r = []
             for e in (0, 1):
                 rows = pl.ds(e, pulses // 2, stride=2)
@@ -1066,9 +1067,8 @@
         def _():
             for i in range(chunk):
                 echo_across((j - lag) * chunk + i).wait_recv()
-            echo_forward(j - lag).start()
-
-    relay(1, 0)
+                echo_forward((j - lag) * chunk + i).start()
+
     scaling_core().wait_recv()
     for copy in get_tables[1:]:
         copy.wait()
@@ -1077,6 +1077,7 @@
     def _(u):
         @pl.when(u == 1)
         def _():
+            relay(1, 0)
             range_chip().wait_recv()
             sideways(az).start()
 
@@ -1172,8 +1173,8 @@
     def _(j):
         for i in range(chunk):
             echo_across(j * chunk + i).wait_send()
+            echo_forward(j * chunk + i).wait_send()
         echo_core(j).wait_send()
-        echo_forward(j).wait_send()
 
     range_chip().wait_send()
     for k in (0, 1):
@@ -1255,7 +1256,7 @@
             dma((n_one,)), dma((n_one,)),
             dma((n_one,)), dma((n_one,)),
             dma((chunks,)), dma((chunks,)),
-            dma((chunks,)), dma((chunks,)),
+            dma((n_one,)), dma((n_one,)),
             dma, dma,
             dma((3,)), dma((3,)),
             dma((n_az, 3)), dma((n_az, 3)), dma((n_az, 3)),

time: 206 us -> 206 us (level)
  no operation moved by 1% of the time
where the time goes in v8:
time: 206 us; the launch traced here: 205 us
  Pallas kernels  203 us (99%)
    pallas_call x1, Pallas kernels, pair_body(): pl.pallas_call(functools.partial(pair_kernel, n_strip, n_az, block, chunk...  203 us

profile of v8, /device:TPU:16, one launch (start us, length us, event | category | flops | bytes accessed | tf_op | source)
XLA Modules:
  0.0 205.0 jit_solution(17704817087736002645)
XLA Ops:
  0.0 203.0 %shard_map.100 = f32[2,512,1024]{2,1,0:T(8,128)S(1)} custom-call(f32[2,128,4096]{2,1,0:T(8,128)} %raw_ref.1, f32[1024,1024]{1,0:T(8,128)} %scaling_ref.1, f32[256,4096]{1,0:T(8,128)} %range_ref.1, f32[1024,1024]{1,0:T(8,128)} %azimuth_ref.1, bf16[2,2,256,512]{3,2,1,0:T(8,128)(2,1)} %constant.12.clone.front_ref, f32[256,128]{1,0:T(8,128)} %constant.13.clone.twists_any, ...), custom_call_target="tpu_custom_call" | custom-call | tf_op jit(solution)/shard_map/pallas_call | solution.py:1227
  203.0 2.0 copy.12
